TPU v7x, 32 devices: a whole 2x2x4 slice. The times are simulated.
32 devices in a mesh: gx: 8 (over z, x), yz: 4 (over y, core).
Axes of the slice: x: 2, y: 2, z: 4, core: 2. Of those that a mesh axis runs over, the one named last changes fastest.
Arguments:
- velocity: bfloat16 [3, 8, 1024, 2048], P(None, 'gx', None, 'yz'), may hold values from -6 to 6
- mean_flow: float32 [1024], replicated, may hold values from 0.5 to 1.5
- chol_diag: float32 [3, 1024], replicated, may hold values from 0.3 to 3
- chol_off: float32 [3, 1024], replicated, may hold values from -3 to 3
- eddy_x: int32 [1536], replicated, may hold values from -64 to 63
- eddy_y: int32 [1536], replicated, may hold values from 0 to 1023
- eddy_z: int32 [1536], replicated, may hold values from 0 to 2047, as said below
- eddy_signs: int32 [3, 1536], replicated, may hold values from 0 to 1
- tile_lists: int32 [16, 288], P('yz'), may hold values from 0 to 1535, as said below
Outputs:
- velocity_next: bfloat16 [3, 8, 1024, 2048], P(None, 'gx', None, 'yz')
- inflow: float32 [1, 3, 1024, 2048], P(None, None, None, 'yz')
Inputs may be any that keep to these rules, and one draw needn't show every extreme that they name: Each tile of 128 spanwise cells is the home of exactly 96 eddies; the home tile of eddy e is eddy_z[e] // 128. `tile_lists`: row t holds, in some order and each once, exactly the eddies whose home tile is t - 1, t or t + 1, counted modulo 16.
All inputs are finite; a program needn't handle non-finite values.
Results may differ from a plain program's by a relative error of at most 0.0047.
Values may be sent and summed in bfloat16 or wider, within the bound.
A program may use at most 192 MiB of HBM per device.

v0:
```python
import math

import jax
import jax.numpy as jnp
import numpy as np
from jax import lax
from jax.experimental import pallas as pl
from jax.experimental.pallas import tpu as pltpu
from jax.sharding import PartitionSpec as P

TILE = 128
EPT = 96
SIGMA = 64
LANES = 128
WINDOW = 128
HALO = 16

shape_peak = math.sqrt(1.5)
time_step = 0.4
viscosity = 0.3
bulk_speed = 1.0


def tent_shape(ratio):
    return shape_peak * jnp.maximum(0.0, 1.0 - jnp.abs(ratio))


def wall_bases(rows):
    inner = 32
    norm = math.sqrt(2.0 / rows)
    y = np.arange(rows)[None, :]
    p = np.arange(rows // inner)[:, None] * inner
    q = np.arange(inner)[:, None]

    def angles(k, position, period):
        return (k * position % period) * (2.0 * math.pi / period)

    def single(table):
        return jnp.asarray(table.astype(np.float32))

    a, b = angles(p, 2 * y + 1, 4 * rows), angles(q, 2 * y + 1, 4 * rows)
    cosine = (
        single(norm * np.cos(a))[:, None] * single(np.cos(b))[None]
        - single(norm * np.sin(a))[:, None] * single(np.sin(b))[None]
    ).reshape(rows, rows)
    cosine = jnp.where(jnp.arange(rows)[:, None] == 0, math.sqrt(1.0 / rows), cosine)
    a, b = angles(p, y + 1, 2 * rows), angles(q, y + 1, 2 * rows)
    sine = (
        single(norm * np.sin(a))[:, None] * single(np.cos(b))[None]
        + single(norm * np.cos(a))[:, None] * single(np.sin(b))[None]
    ).reshape(rows, rows)
    return cosine, sine


def decay_rates(rows):
    return 2.0 * np.arcsinh(np.sin(np.arange(rows) * (math.pi / (2 * rows))))


def line_kernel(f_ref, coef_ref, g_ref, h_ref):
    rate, alpha, beta = coef_ref[0], coef_ref[1], coef_ref[2]
    mean, carry_up, carry_down = coef_ref[3], coef_ref[4], coef_ref[5]
    length = f_ref.shape[0]

    def down(step, carry):
        z = length - 1 - step
        g_ref[z] = carry
        return f_ref[z] - mean + rate * carry

    lax.fori_loop(0, length, down, carry_down, unroll=8)

    def up(z, carry):
        total = f_ref[z] - mean + rate * carry
        after = g_ref[z]
        g_ref[z] = alpha * (total - after)
        h_ref[z] = beta * (total + rate * after)
        return total

    lax.fori_loop(0, length, up, carry_up, unroll=8)


def line_solve(modes, theta, axis, held, forward):
    length, rows = modes.shape
    count = lax.axis_size(axis)
    total = count * length
    me = lax.axis_index(axis)
    short = 32
    outer = np.arange(length // short)[:, None]
    inner = np.arange(short)[:, None]
    blocks = modes.reshape(length // short, short, rows)
    up_out = np.exp(-theta[None] * (length - short - short * outer))
    up_in = np.exp(-theta[None] * (short - 1 - inner))
    down_out = np.exp(-theta[None] * short * outer)
    down_in = np.exp(-theta[None] * inner)
    down_in[:, 0] = inner[:, 0]
    down_out[:, 0] = -1.0
    extra = np.zeros_like(up_out)
    extra[:, 0] = length - short * outer[:, 0]
    table = lambda values: jnp.asarray(values.astype(np.float32))
    part_up = jnp.sum(blocks * table(up_in)[None], axis=1)
    part_down = jnp.sum(blocks * table(down_in)[None], axis=1)
    sums = jnp.stack(
        [
            jnp.sum(part_up * table(up_out), axis=0),
            jnp.sum(part_down * table(down_out) + part_up * table(extra), axis=0),
        ]
    )
    sums, held = lax.optimization_barrier((sums, held))
    onward = forward(held)
    everyone = lax.all_gather(sums, axis)
    place = jnp.arange(count)
    behind = (me - 1 - place) % count
    ahead = (place - me - 1) % count
    theta_line = jnp.asarray((theta * length).astype(np.float32))
    period = jnp.asarray(np.where(theta > 0, 1.0 / np.maximum(-np.expm1(-theta * total), 1e-30), 1.0).astype(np.float32))
    carry_up = period * jnp.sum(everyone[:, 0] * jnp.exp(-theta_line[None] * behind[:, None].astype(jnp.float32)), axis=0)
    carry_down = period * jnp.sum(everyone[:, 1] * jnp.exp(-theta_line[None] * ahead[:, None].astype(jnp.float32)), axis=0)
    first_tot = everyone[:, 0, 0]
    first_run = everyone[:, 1, 0]
    mean = jnp.sum(first_tot) / total
    tot = first_tot - mean * length
    starts = jnp.cumsum(tot) - tot
    shift = -(jnp.sum(first_run - mean * (length * (length + 1) / 2.0)) + length * jnp.sum(starts)) / total
    mine = (place == me).astype(jnp.float32)
    start = jnp.sum(starts * mine) + shift
    is_first = jnp.arange(rows) == 0
    carry_up = jnp.where(is_first, start, carry_up)
    carry_down = jnp.where(is_first, -start - jnp.sum(tot * mine), carry_down)
    means = jnp.where(is_first, mean, 0.0)
    rate = np.exp(-theta)
    fixed = np.stack([rate, rate / (1.0 + rate), np.sqrt(rate) / (1.0 + rate)]).astype(np.float32)
    coef = jnp.concatenate([jnp.asarray(fixed), jnp.stack([means, carry_up, carry_down])], axis=0)
    lanes = (rows // LANES, LANES)
    g, h = pl.pallas_call(
        line_kernel,
        out_shape=[jax.ShapeDtypeStruct((length,) + lanes, jnp.float32)] * 2,
        in_specs=[pl.BlockSpec(memory_space=pltpu.VMEM)] * 2,
        out_specs=[pl.BlockSpec(memory_space=pltpu.VMEM)] * 2,
        compiler_params=pltpu.CompilerParams(vmem_limit_bytes=24 * 1024 * 1024),
        cost_estimate=pl.CostEstimate(
            flops=10 * length * rows, bytes_accessed=12 * length * rows, transcendentals=0
        ),
        name="line_solve",
    )(modes.reshape((length,) + lanes), coef.reshape((6,) + lanes))
    return g.reshape(length, rows), h.reshape(length, rows), held, onward


def march_kernel(level_ref, mean_ref, inlet_ref, far_ref, q0_ref, q1_ref, p0_ref, p1_ref, o0_ref, o1_ref):
    rows = mean_ref.shape[0]
    level = level_ref[0]
    at_inlet = level == 0
    after_inlet = level == 1
    stride = WINDOW - 2 * HALO
    count = -(-(rows - WINDOW) // stride) + 1
    local = lax.broadcasted_iota(jnp.int32, (WINDOW, LANES), 0)

    def window(index, carry):
        start = pl.multiple_of(jnp.minimum(index * stride, rows - WINDOW), HALO)
        here = pl.ds(start, WINDOW)
        low_wall = local + start == 0
        high_wall = local + start == rows - 1
        mean = mean_ref[here, :]
        drag = mean + 2.0 * viscosity

        def load(ref):
            return [ref[c, here, :].astype(jnp.float32) for c in range(3)]

        def rate(field, behind):
            half = 0.5 * field[1]
            up, down = viscosity - half, viscosity + half
            out = []
            for c in range(3):
                above = jnp.where(high_wall, 0.0, jnp.roll(field[c], -1, axis=0))
                below = jnp.where(low_wall, 0.0, jnp.roll(field[c], 1, axis=0))
                out.append(up * above + down * below + mean * behind[c] - drag * field[c])
            return out

        def pick(flag, first, second):
            return [jnp.where(flag, a, b) for a, b in zip(first, second)]

        def rounded(field):
            return [a.astype(jnp.bfloat16).astype(jnp.float32) for a in field]

        def one(field, f0):
            return [u + time_step * (8.0 / 15.0) * a for u, a in zip(field, f0)]

        def two(field, f1, f0):
            return [
                u + (time_step * 5.0 / 12.0) * b - (time_step * 17.0 / 60.0) * a
                for u, b, a in zip(field, f1, f0)
            ]

        def three(field, f2, f1):
            return [
                u + (time_step * 0.75) * b - (time_step * 5.0 / 12.0) * a
                for u, b, a in zip(field, f2, f1)
            ]

        inlet = load(inlet_ref)
        far = pick(after_inlet, inlet, load(far_ref))
        q0, q1, p0, p1 = load(q0_ref), load(q1_ref), load(p0_ref), load(p1_ref)
        q0_1 = rounded(one(q0, rate(q0, far)))
        q1_f0 = rate(q1, q0)
        q1_1 = one(q1, q1_f0)
        q1_2 = rounded(two(q1_1, rate(q1_1, q0_1), q1_f0))
        p0_f0 = rate(p0, pick(at_inlet, inlet, q1))
        p0_1 = one(p0, p0_f0)
        p0_f1 = rate(p0_1, pick(at_inlet, inlet, rounded(q1_1)))
        p0_2 = two(p0_1, p0_f1, p0_f0)
        p0_3 = three(p0_2, rate(p0_2, pick(at_inlet, inlet, q1_2)), p0_f1)
        p1_f0 = rate(p1, p0)
        p1_1 = one(p1, p1_f0)
        p1_f1 = rate(p1_1, rounded(p0_1))
        p1_2 = two(p1_1, p1_f1, p1_f0)
        p1_3 = three(p1_2, rate(p1_2, rounded(p0_2)), p1_f1)
        inner = pl.ds(pl.multiple_of(start + HALO, HALO), WINDOW - HALO)
        results = ((o0_ref, p0_3), (o1_ref, p1_3))
        for ref, value in results:
            for c in range(3):
                ref[c, inner, :] = value[c][HALO:].astype(ref.dtype)

        @pl.when(index == 0)
        def _():
            for ref, value in results:
                for c in range(3):
                    ref[c, 0:HALO, :] = value[c][:HALO].astype(ref.dtype)

        return carry

    lax.fori_loop(0, count, window, 0)


def march(level, mean_lanes, inlet, far, q0, q1, p0, p1):
    shape = p0.shape
    rows = shape[1]
    flops = 9 * 3 * 12 * rows * LANES
    return pl.pallas_call(
        march_kernel,
        out_shape=[jax.ShapeDtypeStruct(shape, jnp.bfloat16)] * 2,
        in_specs=[pl.BlockSpec(memory_space=pltpu.SMEM)] + [pl.BlockSpec(memory_space=pltpu.VMEM)] * 7,
        out_specs=[pl.BlockSpec(memory_space=pltpu.VMEM)] * 2,
        compiler_params=pltpu.CompilerParams(vmem_limit_bytes=28 * 1024 * 1024),
        cost_estimate=pl.CostEstimate(flops=flops, bytes_accessed=16 * 3 * rows * LANES, transcendentals=0),
        name="march",
    )(level, mean_lanes, inlet, far, q0, q1, p0, p1)


def inlet_planes(mean_flow, chol_diag, chol_off, eddy_x, eddy_y, eddy_z, eddy_signs, columns, spanwise, held, forward):
    rows = mean_flow.shape[0]
    first_cell = lax.axis_index("yz") * columns
    signs = (2 * eddy_signs - 1).astype(jnp.float32)
    cells_y = jnp.arange(rows, dtype=jnp.int32)
    shape_y = tent_shape((cells_y[None, :] - eddy_y[:, None]).astype(jnp.float32) / SIGMA).astype(jnp.bfloat16)
    amplitude = math.sqrt(8.0 * rows / (TILE * EPT))
    scale = (amplitude * tent_shape(eddy_x.astype(jnp.float32) / SIGMA))[None, :] * signs

    def fluct_at(cells):
        offset = (cells[None, :] - eddy_z[:, None] + spanwise // 2) % spanwise - spanwise // 2
        shape_z = tent_shape(offset.astype(jnp.float32) / SIGMA)
        weight = (scale[:, :, None] * shape_z[None]).astype(jnp.bfloat16)
        return jnp.einsum("ey,jez->jyz", shape_y, weight, preferred_element_type=jnp.float32)

    fluct = fluct_at(first_cell + jnp.arange(columns, dtype=jnp.int32))
    edge = fluct_at((first_cell - 1 + spanwise) % spanwise + jnp.arange(1, dtype=jnp.int32))

    def mix(fl):
        return chol_off[1][:, None] * fl[0] + chol_off[2][:, None] * fl[1] + chol_diag[2][:, None] * fl[2]

    first = mean_flow[:, None] + chol_diag[0][:, None] * fluct[0]
    second = chol_off[0][:, None] * fluct[0] + chol_diag[1][:, None] * fluct[1]
    third = mix(fluct)
    flux = second * (cells_y < rows - 1).astype(jnp.float32)[:, None]
    lower = jnp.concatenate([jnp.zeros_like(flux[:1]), flux[:-1]], axis=0)
    previous = jnp.concatenate([mix(edge), third[:, :-1]], axis=1)
    div = flux - lower + third - previous
    high = lax.Precision.HIGH
    cosine, sine = wall_bases(rows)
    modes = jnp.einsum("yz,ky->zk", div, cosine, precision=high)
    slope_modes, rise_modes, held, onward = line_solve(modes, decay_rates(rows), "yz", held, forward)
    slope = jnp.einsum(
        "ky,zk->yz", cosine.astype(jnp.bfloat16), slope_modes.astype(jnp.bfloat16), preferred_element_type=jnp.float32
    )
    rise = jnp.einsum(
        "ky,zk->yz", sine.astype(jnp.bfloat16), rise_modes.astype(jnp.bfloat16), preferred_element_type=jnp.float32
    )
    return jnp.stack([first, flux - rise, third - slope], axis=0), held, onward


def body(velocity, mean_flow, chol_diag, chol_off, eddy_x, eddy_y, eddy_z, eddy_signs, tile_lists):
    rows, columns = velocity.shape[2:]
    spanwise = columns * lax.axis_size("yz")
    slabs = lax.axis_size("gx")
    plane = velocity[:, 0]
    me = lax.axis_index("gx")
    even = me % 2 == 0
    half = columns // 2
    swap = [(i, i ^ 1) for i in range(slabs)]
    onward = [(i, i + 2) for i in range(slabs - 2)]
    low, high = plane[:, :, :half], plane[:, :, half:]
    keep = jnp.where(even, low, high)
    other = lax.ppermute(jnp.where(even, high, low), "gx", swap)
    near = lax.ppermute(keep, "gx", onward)

    def forward(held):
        return lax.ppermute(held[0], "gx", onward)

    inflow, (other, near), next_near = inlet_planes(
        mean_flow, chol_diag, chol_off, eddy_x, eddy_y, eddy_z, eddy_signs, columns, spanwise, (other, near), forward
    )
    inflow, next_near = lax.optimization_barrier((inflow, next_near))
    p0 = jnp.where(even, keep, other)
    p1 = jnp.where(even, other, keep)
    q0 = jnp.where(even, near, next_near)
    q1 = jnp.where(even, next_near, near)
    chunks = []
    for begin in range(0, half, LANES):
        cut = [value[:, :, begin : begin + LANES] for value in (q0, q1, p0, p1)]
        chunks.append((lax.ppermute(cut[1], "gx", onward), *cut))
    mean_lanes = jnp.broadcast_to(mean_flow[:, None], (rows, LANES))
    level = (me // 2).astype(jnp.int32).reshape(1)
    lows, highs = [], []
    for number, planes in enumerate(chunks):
        begin = number * LANES
        inlet = jnp.where(
            even, inflow[:, :, begin : begin + LANES], inflow[:, :, half + begin : half + begin + LANES]
        ).astype(jnp.bfloat16)
        o0, o1 = march(level, mean_lanes, inlet, *planes)
        keep = jnp.where(even, o0, o1)
        other = lax.ppermute(jnp.where(even, o1, o0), "gx", swap)
        lows.append(jnp.where(even, keep, other))
        highs.append(jnp.where(even, other, keep))
    velocity_next = jnp.concatenate(lows + highs, axis=2)[:, None]
    return (velocity_next, inflow[None])


def solution(mesh):
    placed = (P(None, "gx", None, "yz"), P(), P(), P(), P(), P(), P(), P(), P("yz", None))
    return jax.shard_map(
        body,
        mesh=mesh,
        in_specs=placed,
        out_specs=(P(None, "gx", None, "yz"), P(None, None, None, "yz")),
        check_vma=False,
    )
```

profile of v0, /device:TPU:8, one launch (start us, length us, event | category | flops | bytes accessed | tf_op | source)
XLA Modules:
  0.0 168.2 jit_solution(1963681762174447038)
XLA Ops:
  0.7 3.7 %broadcast_select_fusion.4 = (bf16[3,1024,256]{2,1,0:T(8,128)(2,1)}, bf16[3,1024,256]{2,1,0:T(8,128)(2,1)}) fusion(pred[]{:T(512)S(6)} %eq.53, bf16[3,1024,512]{2,1,0:T(8,128)(2,1)} %bitcast.100), kind=kLoop, calls=%fused_computation.52 | loop fusion | flops 1572864 | bytes 6291457 | tf_op jit(solution)/shard_map/jit(_where)/select_n | solution.py:299
  4.4 1.5 collective-permute-start
  5.9 3.5 %collective-permute-start.1 = (bf16[3,1024,256]{2,1,0:T(8,128)(2,1)}, bf16[3,1024,256]{2,1,0:T(8,128)(2,1)}, u32[]{:S(2)}, u32[]{:S(2)}) collective-permute-start(bf16[3,1024,256]{2,1,0:T(8,128)(2,1)} %get-tuple-element.53), channel_id=1, source_target_pairs={{0,8},{4,12},{8,16},{12,20},{16,24},{20,28},{1,9},{5,13},{9,17},{1... | collective-permute-start | bytes 4718600 | tf_op jit(solution)/shard_map/ppermute | solution.py:301
  9.4 2.1 %fusion.10 = f32[1536,512]{0,1:T(8,128)S(1)} fusion(s32[1536]{0:T(1024)S(1)} %copy-done.22, s32[512]{0:T(512)S(1)} %iota_add_fusion), kind=kLoop, calls=%fused_computation.20 | loop fusion | flops 15728640 | bytes 3153920 | tf_op jit(solution)/shard_map/mul | solution.py:25
  11.7 6.1 %fusion.13 = f32[3,1024,512]{2,1,0:T(8,128)S(1)} fusion(s32[1536]{0:T(1024)S(1)} %copy-done.31, f32[1536,512]{0,1:T(8,128)S(1)} %fusion.10, f32[3,1536]{1,0:T(4,128)S(1)} %convert_multiply_fusion), kind=kOutput, calls=%fused_computation.24 | convolution fusion | flops 4849139712 | bytes 9461760 | tf_op jit(solution)/shard_map/ey,jez->jyz/dot_general | solution.py:260
  17.8 1.8 %fusion.12 = f32[3,1024]{1,0:T(4,128)S(1)} fusion(s32[1536]{0:T(1024)S(1)} %copy-done.31, f32[3,1536]{1,0:T(4,128)S(1)} %convert_multiply_fusion, f32[1536]{0:T(1024)S(1)} %fusion.42), kind=kOutput, calls=%fused_computation.23 | convolution fusion | flops 22029312 | bytes 43008 | tf_op jit(solution)/shard_map/ey,jez->jyz/dot_general | solution.py:260
  19.7 3.4 %multiply_subtract_fusion = (f32[32,32,1024]{2,1,0:T(8,128)}, bf16[32,32,1024]{2,1,0:T(8,128)(2,1)}) fusion(f32[32,1024]{1,0:T(8,128)S(1)} %copy-done.15, f32[32,1024]{1,0:T(8,128)S(1)} %copy-done.16, f32[32,1024]{1,0:T(8,128)S(1)} %copy-done.17, f32[32,1024]{1,0:T(8,128)S(1)} %copy-done.18, pred[32,32]{1,0:T(8,128)(4,1)S(1)} %add_compare_fusion), kind=kLoop, calls=%fused_computation.11 | loop fusion | flops 5242880 | bytes 6816768 | tf_op jit(solution)/shard_map/sub | solution.py:43
  23.1 2.5 %fusion.22 = (f32[1024,512]{1,0:T(8,128)S(1)}, f32[1024,512]{1,0:T(8,128)}) fusion(f32[3,1024,512]{2,1,0:T(8,128)S(1)} %fusion.13, f32[1024]{0:T(1024)S(1)} %fusion.46, f32[1024]{0:T(1024)S(1)} %bitcast.110, f32[1024]{0:T(1024)S(1)} %bitcast.106, f32[1024]{0:T(1024)S(1)} %bitcast.109, f32[1024]{0:T(1024)S(1)} %bitcast.107, f32[1024]{0:T(1024)S(1)} %bitcast.108), kind=kLoop, calls=%fused_computation.36 | loop fusion | flops 4718592 | bytes 10510336 | tf_op jit(solution)/shard_map/mul | solution.py:271
  25.9 3.1 %bitcast_select_fusion = f32[1024,1024]{1,0:T(8,128)S(1)} fusion(f32[32,32,1024]{2,1,0:T(8,128)} %get-tuple-element.67, pred[1024]{0:T(1024)(128)(4,1)S(1)} %iota_compare_fusion), kind=kLoop, calls=%fused_computation.9 | loop fusion | flops 1048576 | bytes 8389632 | tf_op jit(solution)/shard_map/jit(_where)/select_n | solution.py:46
  29.2 7.8 %multiply_reduce_fusion = (f32[16,1024]{1,0:T(8,128)S(1)}, f32[16,1024]{1,0:T(8,128)S(1)}, f32[512,1024]{1,0:T(8,128)S(1)}) fusion(f32[32,1024]{1,0:T(8,128)S(1)} %copy-done.9, f32[32,1024]{1,0:T(8,128)S(1)} %copy-done.10, f32[1024,1024]{1,0:T(8,128)S(1)} %bitcast_select_fusion, f32[1024,511]{1,0:T(8,128)S(1)} %bitcast.97, f32[1024,1]{1,0:T(8,128)S(1)} %copy.41, ...), kind=kOutput, calls=%fused_computation.40 | convolution fusion | flops 3225387008 | bytes 15071232 | tf_op jit(solution)/shard_map/yz,ky->zk/dot_general | solution.py:277
  38.3 2.0 %add_convert_fusion = bf16[32,32,1024]{2,1,0:T(8,128)(2,1)} fusion(f32[32,1024]{1,0:T(8,128)S(1)} %copy-done.11, f32[32,1024]{1,0:T(8,128)S(1)} %copy-done.12, f32[32,1024]{1,0:T(8,128)S(1)} %copy-done.13, f32[32,1024]{1,0:T(8,128)S(1)} %copy-done.14), kind=kLoop, calls=%fused_computation.12 | loop fusion | flops 4194304 | bytes 2621440 | tf_op jit(solution)/shard_map/convert_element_type | solution.py:283
  40.2 3.2 %multiply_add_fusion = f32[1,1024,512]{2,1,0:T(8,128)} fusion(f32[3,1024,512]{2,1,0:T(8,128)} %copy-done.5, f32[1024]{0:T(1024)S(1)} %bitcast.113, f32[1024]{0:T(1024)S(1)} %copy-done.24), kind=kLoop, calls=%fused_computation.45 | loop fusion | flops 1048576 | bytes 4202496 | tf_op jit(solution)/shard_map/add | solution.py:268
  43.9 5.2 %all-gather.1 = f32[4,2,1024]{2,1,0:T(2,128)S(1)} all-gather(f32[1,2,1024]{2,1,0:T(2,128)S(1)} %bitcast.105), channel_id=2, replica_groups=mesh['gx'=8,'yz'=4] {'yz'}, dimensions={0}, use_global_device_ids=true | all-gather | bytes 40960 | tf_op jit(solution)/shard_map/all_gather | solution.py:109
  55.1 3.5 %collective-permute-start.2 = (bf16[3,1024,256]{2,1,0:T(8,128)(2,1)}, bf16[3,1024,256]{2,1,0:T(8,128)(2,1)}, u32[]{:S(2)}, u32[]{:S(2)}) collective-permute-start(bf16[3,1024,256]{2,1,0:T(8,128)(2,1)} %collective-permute-done), channel_id=1, source_target_pairs={{0,8},{4,12},{8,16},{12,20},{16,24},{20,28},{1,9},{5,13},{9,17},{1... | collective-permute-start | bytes 4718600 | tf_op jit(solution)/shard_map/ppermute | solution.py:304
  59.4 2.7 %line_solve.1 = (f32[512,8,128]{2,1,0:T(8,128)S(1)}, f32[512,8,128]{2,1,0:T(8,128)S(1)}) custom-call(f32[512,8,128]{2,1,0:T(8,128)S(1)} %bitcast.95, f32[6,8,128]{2,1,0:T(8,128)S(1)} %pad_maximum_fusion.1.coef_ref), custom_call_target="tpu_custom_call" | custom-call | flops 5242880 | bytes 6291456 | tf_op jit(solution)/shard_map/line_solve/pallas_call | solution.py:133
  62.3 1.3 copy-done.3
  64.3 1.3 subtract_bitcast_fusion
  66.5 1.3 subtract_bitcast_fusion.1
  68.1 0.7 pad_maximum_fusion
  68.8 4.4 %broadcast_select_fusion = (bf16[3,1024,256]{2,1,0:T(8,128)(2,1)S(1)}, bf16[3,1024,256]{2,1,0:T(8,128)(2,1)S(1)}) fusion(bf16[3,1024,256]{2,1,0:T(8,128)(2,1)} %collective-permute-done, bf16[3,1024,256]{2,1,0:T(8,128)(2,1)} %get-tuple-element.53, pred[]{:T(512)S(6)} %eq.53), kind=kLoop, calls=%fused_computation.48 | loop fusion | flops 1572864 | bytes 6291457 | tf_op jit(solution)/shard_map/jit(_where)/select_n | solution.py:311
  73.2 20.7 %collective-permute-done.2 = bf16[3,1024,256]{2,1,0:T(8,128)(2,1)} collective-permute-done((bf16[3,1024,256]{2,1,0:T(8,128)(2,1)}, bf16[3,1024,256]{2,1,0:T(8,128)(2,1)}, u32[]{:S(2)}, u32[]{:S(2)}) %collective-permute-start.2) | collective-permute-done | bytes 1572896 | tf_op jit(solution)/shard_map/ppermute | solution.py:304
  93.9 2.1 %broadcast_select_fusion.2 = (bf16[3,1024,256]{2,1,0:T(8,128)(2,1)S(1)}, bf16[3,1024,256]{2,1,0:T(8,128)(2,1)S(1)}) fusion(bf16[3,1024,256]{2,1,0:T(8,128)(2,1)} %collective-permute-done.1, bf16[3,1024,256]{2,1,0:T(8,128)(2,1)} %collective-permute-done.2, pred[]{:T(512)S(6)} %eq.53), kind=kLoop, calls=%fused_computation.50 | loop fusion | flops 1572864 | bytes 6291457 | tf_op jit(solution)/shard_map/jit(_where)/select_n | solution.py:312
  96.3 3.5 %collective-permute-start.5 = (bf16[3,1024,128]{2,1,0:T(8,128)(2,1)S(1)}, bf16[3,1024,128]{2,1,0:T(8,128)(2,1)S(1)}, u32[]{:S(2)}, u32[]{:S(2)}) collective-permute-start(bf16[3,1024,128]{2,1,0:T(8,128)(2,1)S(1)} %get-tuple-element.66.q1_ref), channel_id=1, source_target_pairs={{0,8},{4,12},{8,16},{12,20},{16,24},{20,28},{1,9},{5,13},{9,17},{1... | collective-permute-start | bytes 2359304 | tf_op jit(solution)/shard_map/ppermute | solution.py:317
  99.8 0.7 fusion.66
  100.5 3.5 %collective-permute-start.3 = (bf16[3,1024,128]{2,1,0:T(8,128)(2,1)S(1)}, bf16[3,1024,128]{2,1,0:T(8,128)(2,1)S(1)}, u32[]{:S(2)}, u32[]{:S(2)}) collective-permute-start(bf16[3,1024,128]{2,1,0:T(8,128)(2,1)S(1)} %get-tuple-element.65.q1_ref), channel_id=1, source_target_pairs={{0,8},{4,12},{8,16},{12,20},{16,24},{20,28},{1,9},{5,13},{9,17},{1... | collective-permute-start | bytes 2359304 | tf_op jit(solution)/shard_map/ppermute | solution.py:317
  104.6 14.1 %collective-permute-done.5.far_ref = bf16[3,1024,128]{2,1,0:T(8,128)(2,1)S(1)} collective-permute-done((bf16[3,1024,128]{2,1,0:T(8,128)(2,1)S(1)}, bf16[3,1024,128]{2,1,0:T(8,128)(2,1)S(1)}, u32[]{:S(2)}, u32[]{:S(2)}) %collective-permute-start.5) | collective-permute-done | bytes 786464 | tf_op jit(solution)/shard_map/ppermute | solution.py:317
  118.9 13.8 %march.3 = (bf16[3,1024,128]{2,1,0:T(8,128)(2,1)S(1)}, bf16[3,1024,128]{2,1,0:T(8,128)(2,1)S(1)}) custom-call(s32[1]{0:T(128)} %bitcast.level_ref, f32[1024,128]{1,0:T(8,128)S(1)} %broadcast_in_dim.34.mean_ref, bf16[3,1024,128]{2,1,0:T(8,128)(2,1)S(1)} %get-tuple-element.46.inlet_ref, bf16[3,1024,128]{2,1,0:T(8,128)(2,1)S(1)} %collective-permute-done.5.far_ref, ...), custom_call_target="tpu_custom_call" | custom-call | flops 42467328 | bytes 6291456 | tf_op jit(solution)/shard_map/march/pallas_call | solution.py:236
  134.0 13.8 %march.2 = (bf16[3,1024,128]{2,1,0:T(8,128)(2,1)S(1)}, bf16[3,1024,128]{2,1,0:T(8,128)(2,1)S(1)}) custom-call(s32[1]{0:T(128)} %bitcast.level_ref, f32[1024,128]{1,0:T(8,128)S(1)} %broadcast_in_dim.34.mean_ref, bf16[3,1024,128]{2,1,0:T(8,128)(2,1)S(1)} %get-tuple-element.45.inlet_ref, bf16[3,1024,128]{2,1,0:T(8,128)(2,1)S(1)} %collective-permute-done.3.far_ref, ...), custom_call_target="tpu_custom_call" | custom-call | flops 42467328 | bytes 6291456 | tf_op jit(solution)/shard_map/march/pallas_call | solution.py:236
  147.9 0.9 collective-permute-start.4
  148.8 0.7 collective-permute-done.6
  149.7 16.5 %collective-permute-done.4 = bf16[3,1024,128]{2,1,0:T(8,128)(2,1)S(1)} collective-permute-done((bf16[3,1024,128]{2,1,0:T(8,128)(2,1)S(1)}, bf16[3,1024,128]{2,1,0:T(8,128)(2,1)S(1)}, u32[]{:S(2)}, u32[]{:S(2)}) %collective-permute-start.4) | collective-permute-done | bytes 786464 | tf_op jit(solution)/shard_map/ppermute | solution.py:328
  166.3 1.9 %maximum_bitcast_fusion = bf16[3,1,1024,512]{3,2,1,0:T(8,128)(2,1)} fusion(bf16[3,1024,128]{2,1,0:T(8,128)(2,1)S(1)} %get-tuple-element.58, bf16[3,1024,128]{2,1,0:T(8,128)(2,1)S(1)} %get-tuple-element.56, bf16[3,1024,128]{2,1,0:T(8,128)(2,1)S(1)} %get-tuple-element.57, bf16[3,1024,128]{2,1,0:T(8,128)(2,1)S(1)} %get-tuple-element.55), kind=kLoop, calls=%fused_computation.21 | loop fusion | flops 12582912 | bytes 6291456
  (99 shorter events, 9.3 us)
Async XLA Ops:
  0.6 8.8 %copy-start.28 = (s32[1536]{0:T(1024)S(1)}, s32[1536]{0:T(1024)}, u32[]{:S(2)}) copy-start(s32[1536]{0:T(1024)} %param.29) | copy-start | bytes 18436
  0.7 8.8 %copy-start.22 = (s32[1536]{0:T(1024)S(1)}, s32[1536]{0:T(1024)}, u32[]{:S(2)}) copy-start(s32[1536]{0:T(1024)} %param.31) | copy-start | bytes 18436
  4.4 7.2 %copy-start.23 = (s32[3,1536]{1,0:T(4,128)S(1)}, s32[3,1536]{1,0:T(4,128)}, u32[]{:S(2)}) copy-start(s32[3,1536]{1,0:T(4,128)} %param.32) | copy-start | bytes 55300
  4.4 7.3 %copy-start.31 = (s32[1536]{0:T(1024)S(1)}, s32[1536]{0:T(1024)}, u32[]{:S(2)}) copy-start(s32[1536]{0:T(1024)} %param.30) | copy-start | bytes 18436
  4.4 39.1 %collective-permute-start = (bf16[3,1024,256]{2,1,0:T(8,128)(2,1)}, bf16[3,1024,256]{2,1,0:T(8,128)(2,1)}, u32[]{:S(2)}, u32[]{:S(2)}) collective-permute-start(bf16[3,1024,256]{2,1,0:T(8,128)(2,1)} %get-tuple-element.54), channel_id=1, source_target_pairs={{0,4},{4,0},{8,12},{12,8},{16,20},{20,16},{24,28},{28,24},{1,5},{5... | collective-permute-start | bytes 4718600 | tf_op jit(solution)/shard_map/ppermute | solution.py:300
  5.9 38.1 %collective-permute-start.1 = (bf16[3,1024,256]{2,1,0:T(8,128)(2,1)}, bf16[3,1024,256]{2,1,0:T(8,128)(2,1)}, u32[]{:S(2)}, u32[]{:S(2)}) collective-permute-start(bf16[3,1024,256]{2,1,0:T(8,128)(2,1)} %get-tuple-element.53), channel_id=1, source_target_pairs={{0,8},{4,12},{8,16},{12,20},{16,24},{20,28},{1,9},{5,13},{9,17},{1... | collective-permute-start | bytes 4718600 | tf_op jit(solution)/shard_map/ppermute | solution.py:301
  17.7 5.3 %copy-start.5 = (f32[3,1024,512]{2,1,0:T(8,128)}, f32[3,1024,512]{2,1,0:T(8,128)S(1)}, u32[]{:S(2)}) copy-start(f32[3,1024,512]{2,1,0:T(8,128)S(1)} %fusion.13) | copy-start | bytes 18874372
  17.8 1.9 %copy-start.26 = (f32[3,1024]{1,0:T(4,128)S(1)}, f32[3,1024]{1,0:T(4,128)}, u32[]{:S(2)}) copy-start(f32[3,1024]{1,0:T(4,128)} %param.27) | copy-start | bytes 36868
  17.8 1.9 %copy-start.27 = (f32[3,1024]{1,0:T(4,128)S(1)}, f32[3,1024]{1,0:T(4,128)}, u32[]{:S(2)}) copy-start(f32[3,1024]{1,0:T(4,128)} %param.28) | copy-start | bytes 36868
  17.8 1.9 %copy-start.15 = (f32[32,1024]{1,0:T(8,128)S(1)}, f32[32,1024]{1,0:T(8,128)}, u32[]{:S(2)}) copy-start(f32[32,1024]{1,0:T(8,128)} %constant.186.clone) | copy-start | bytes 393220
  17.8 1.9 %copy-start.16 = (f32[32,1024]{1,0:T(8,128)S(1)}, f32[32,1024]{1,0:T(8,128)}, u32[]{:S(2)}) copy-start(f32[32,1024]{1,0:T(8,128)} %constant.185.clone) | copy-start | bytes 393220
  17.8 1.9 %copy-start.17 = (f32[32,1024]{1,0:T(8,128)S(1)}, f32[32,1024]{1,0:T(8,128)}, u32[]{:S(2)}) copy-start(f32[32,1024]{1,0:T(8,128)} %constant.184.clone) | copy-start | bytes 393220
  17.8 1.9 %copy-start.18 = (f32[32,1024]{1,0:T(8,128)S(1)}, f32[32,1024]{1,0:T(8,128)}, u32[]{:S(2)}) copy-start(f32[32,1024]{1,0:T(8,128)} %constant.183.clone) | copy-start | bytes 393220
  25.6 3.4 %copy-start = (f32[1024,512]{1,0:T(8,128)}, f32[1024,512]{1,0:T(8,128)S(1)}, u32[]{:S(2)}) copy-start(f32[1024,512]{1,0:T(8,128)S(1)} %get-tuple-element.47) | copy-start | bytes 6291460
  25.9 3.4 %copy-start.2 = (f32[1024,512]{1,0:T(8,128)S(1)}, f32[1024,512]{1,0:T(8,128)}, u32[]{:S(2)}) copy-start(f32[1024,512]{1,0:T(8,128)} %get-tuple-element.48) | copy-start | bytes 6291460
  25.9 3.4 %copy-start.9 = (f32[32,1024]{1,0:T(8,128)S(1)}, f32[32,1024]{1,0:T(8,128)}, u32[]{:S(2)}) copy-start(f32[32,1024]{1,0:T(8,128)} %constant.192.clone) | copy-start | bytes 393220
  25.9 3.3 %copy-start.10 = (f32[32,1024]{1,0:T(8,128)S(1)}, f32[32,1024]{1,0:T(8,128)}, u32[]{:S(2)}) copy-start(f32[32,1024]{1,0:T(8,128)} %constant.191.clone) | copy-start | bytes 393220
  37.1 3.1 %copy-start.24 = (f32[1024]{0:T(1024)S(1)}, f32[1024]{0:T(1024)}, u32[]{:S(2)}) copy-start(f32[1024]{0:T(1024)} %param.26) | copy-start | bytes 12292
  38.3 21.0 %copy-start.29 = (f32[1024]{0:T(1024)S(1)}, f32[1024]{0:T(1024)}, u32[]{:S(2)}) copy-start(f32[1024]{0:T(1024)} %constant.203) | copy-start | bytes 12292
  38.3 21.1 %copy-start.30 = (f32[1024]{0:T(1024)S(1)}, f32[1024]{0:T(1024)}, u32[]{:S(2)}) copy-start(f32[1024]{0:T(1024)} %constant.197.clone) | copy-start | bytes 12292
  38.3 21.1 %copy-start.25 = (f32[3,8,128]{2,1,0:T(8,128)S(1)}, f32[3,8,128]{2,1,0:T(8,128)}, u32[]{:S(2)}) copy-start(f32[3,8,128]{2,1,0:T(8,128)} %constant.202) | copy-start | bytes 36868
  55.1 38.8 %collective-permute-start.2 = (bf16[3,1024,256]{2,1,0:T(8,128)(2,1)}, bf16[3,1024,256]{2,1,0:T(8,128)(2,1)}, u32[]{:S(2)}, u32[]{:S(2)}) collective-permute-start(bf16[3,1024,256]{2,1,0:T(8,128)(2,1)} %collective-permute-done), channel_id=1, source_target_pairs={{0,8},{4,12},{8,16},{12,20},{16,24},{20,28},{1,9},{5,13},{9,17},{1... | collective-permute-start | bytes 4718600 | tf_op jit(solution)/shard_map/ppermute | solution.py:304
  62.1 1.6 copy-start.3
  62.1 2.2 %copy-start.7 = (bf16[32,32,1024]{2,1,0:T(8,128)(2,1)S(1)}, bf16[32,32,1024]{2,1,0:T(8,128)(2,1)}, u32[]{:S(2)}) copy-start(bf16[32,32,1024]{2,1,0:T(8,128)(2,1)} %get-tuple-element.68) | copy-start | bytes 6291460
  64.3 1.6 copy-start.1
  64.3 2.2 %copy-start.8 = (bf16[32,32,1024]{2,1,0:T(8,128)(2,1)S(1)}, bf16[32,32,1024]{2,1,0:T(8,128)(2,1)}, u32[]{:S(2)}) copy-start(bf16[32,32,1024]{2,1,0:T(8,128)(2,1)} %add_convert_fusion) | copy-start | bytes 6291460
  66.5 1.6 copy-start.6
  68.8 35.5 %copy-start.4 = (f32[3,1024,512]{2,1,0:T(8,128)}, f32[3,1024,512]{2,1,0:T(8,128)S(1)}, u32[]{:S(2)}) copy-start(f32[3,1024,512]{2,1,0:T(8,128)S(1)} %pad_maximum_fusion) | copy-start | bytes 18874372
  96.3 22.4 %collective-permute-start.5 = (bf16[3,1024,128]{2,1,0:T(8,128)(2,1)S(1)}, bf16[3,1024,128]{2,1,0:T(8,128)(2,1)S(1)}, u32[]{:S(2)}, u32[]{:S(2)}) collective-permute-start(bf16[3,1024,128]{2,1,0:T(8,128)(2,1)S(1)} %get-tuple-element.66.q1_ref), channel_id=1, source_target_pairs={{0,8},{4,12},{8,16},{12,20},{16,24},{20,28},{1,9},{5,13},{9,17},{1... | collective-permute-start | bytes 2359304 | tf_op jit(solution)/shard_map/ppermute | solution.py:317
  100.5 33.5 %collective-permute-start.3 = (bf16[3,1024,128]{2,1,0:T(8,128)(2,1)S(1)}, bf16[3,1024,128]{2,1,0:T(8,128)(2,1)S(1)}, u32[]{:S(2)}, u32[]{:S(2)}) collective-permute-start(bf16[3,1024,128]{2,1,0:T(8,128)(2,1)S(1)} %get-tuple-element.65.q1_ref), channel_id=1, source_target_pairs={{0,8},{4,12},{8,16},{12,20},{16,24},{20,28},{1,9},{5,13},{9,17},{1... | collective-permute-start | bytes 2359304 | tf_op jit(solution)/shard_map/ppermute | solution.py:317
  132.7 16.7 %collective-permute-start.6 = (bf16[3,1024,128]{2,1,0:T(8,128)(2,1)S(1)}, bf16[3,1024,128]{2,1,0:T(8,128)(2,1)S(1)}, u32[]{:S(2)}, u32[]{:S(2)}) collective-permute-start(bf16[3,1024,128]{2,1,0:T(8,128)(2,1)S(1)} %broadcast_select_fusion.9), channel_id=1, source_target_pairs={{0,4},{4,0},{8,12},{12,8},{16,20},{20,16},{24,28},{28,24},{1,5},{5... | collective-permute-start | bytes 2359304 | tf_op jit(solution)/shard_map/ppermute | solution.py:328
  147.9 18.3 %collective-permute-start.4 = (bf16[3,1024,128]{2,1,0:T(8,128)(2,1)S(1)}, bf16[3,1024,128]{2,1,0:T(8,128)(2,1)S(1)}, u32[]{:S(2)}, u32[]{:S(2)}) collective-permute-start(bf16[3,1024,128]{2,1,0:T(8,128)(2,1)S(1)} %broadcast_select_fusion.12), channel_id=1, source_target_pairs={{0,4},{4,0},{8,12},{12,8},{16,20},{20,16},{24,28},{28,24},{1,5},{5... | collective-permute-start | bytes 2359304 | tf_op jit(solution)/shard_map/ppermute | solution.py:328
  (7 other events, 6.8 us)
where the time goes:
time: 169 us; the launch traced here: 168 us
  waiting for transfers between devices  53.2 us (31%)
  other arithmetic  32.4 us (19%)
  Pallas kernels  30.2 us (18%)
  matrix products  18.3 us (11%)
  starting transfers between devices  16.9 us (10%)
  local copies, waits for them, and re-layouts  6.28 us (4%)
  between operations  5.71 us (3%)
  blocking collectives  5.18 us (3%)
    pallas_call x2, Pallas kernels, march(): pl.pallas_call(march_kernel, out_shape=[jax.ShapeDtypeStruct(shape, jnp.b...  27.5 us
    ppermute x1, waiting for transfers between devices, forward(): return lax.ppermute(held[0], 'gx', onward)  20.7 us
    ppermute x2, waiting for transfers between devices, body(): other = lax.ppermute(jnp.where(even, o1, o0), 'gx', swap)  17.2 us
    ppermute x2, waiting for transfers between devices, body(): chunks.append((lax.ppermute(cut[1], 'gx', onward), *cut))  14.7 us
    dot_general x2, matrix products, fluct_at(): jnp.einsum('ey,jez->jyz', shape_y, weight, preferred_element_type=jnp.flo...  7.9 us
    dot_general x1, matrix products, inlet_planes(): modes = jnp.einsum('yz,ky->zk', div, cosine, precision=high)  7.8 us
    ppermute x2, starting transfers between devices, body(): chunks.append((lax.ppermute(cut[1], 'gx', onward), *cut))  6.97 us
    all_gather x1, blocking collectives, line_solve(): everyone = lax.all_gather(sums, axis)  5.18 us
  transfers between devices with their start and end apart: 7, of which 6 were waited for; matrix products, arithmetic and copies ran while one was open for 25% of the time, Pallas kernels for 18%

commit v1 on v0

--- a/solution.py
+++ b/solution.py
@@ -1,3 +1,4 @@
+import functools
 import math
 
 import jax
@@ -12,8 +13,10 @@
 EPT = 96
 SIGMA = 64
 LANES = 128
-WINDOW = 128
+STRIDE = 128
 HALO = 16
+WINDOW = STRIDE + 2 * HALO
+MESH = pl.DeviceIdType.MESH
 
 shape_peak = math.sqrt(1.5)
 time_step = 0.4
@@ -98,14 +101,14 @@
     table = lambda values: jnp.asarray(values.astype(np.float32))
     part_up = jnp.sum(blocks * table(up_in)[None], axis=1)
     part_down = jnp.sum(blocks * table(down_in)[None], axis=1)
+    part_up, part_down, held = lax.optimization_barrier((part_up, part_down, held))
+    onward = forward(held)
     sums = jnp.stack(
         [
             jnp.sum(part_up * table(up_out), axis=0),
             jnp.sum(part_down * table(down_out) + part_up * table(extra), axis=0),
         ]
     )
-    sums, held = lax.optimization_barrier((sums, held))
-    onward = forward(held)
     everyone = lax.all_gather(sums, axis)
     place = jnp.arange(count)
     behind = (me - 1 - place) % count
@@ -129,6 +132,7 @@
     rate = np.exp(-theta)
     fixed = np.stack([rate, rate / (1.0 + rate), np.sqrt(rate) / (1.0 + rate)]).astype(np.float32)
     coef = jnp.concatenate([jnp.asarray(fixed), jnp.stack([means, carry_up, carry_down])], axis=0)
+    coef, onward = lax.optimization_barrier((coef, onward))
     lanes = (rows // LANES, LANES)
     g, h = pl.pallas_call(
         line_kernel,
@@ -144,104 +148,200 @@
     return g.reshape(length, rows), h.reshape(length, rows), held, onward
 
 
-def march_kernel(level_ref, mean_ref, inlet_ref, far_ref, q0_ref, q1_ref, p0_ref, p1_ref, o0_ref, o1_ref):
+def march_kernel(
+    slabs, mean_ref, inlet_ref, keep_ref, other_ref, near_ref, next_ref,
+    mine_ref, theirs_ref,
+    far, back, far_send, far_recv, back_send, back_recv,
+):
     rows = mean_ref.shape[0]
-    level = level_ref[0]
-    at_inlet = level == 0
-    after_inlet = level == 1
-    stride = WINDOW - 2 * HALO
-    count = -(-(rows - WINDOW) // stride) + 1
+    blocks = rows // STRIDE
+    me = lax.axis_index("gx")
+    even = me % 2 == 0
+    partner = me + 1 - 2 * (me % 2)
+    has_after = me + 2 < slabs
+    has_before = me >= 2
+    after = jnp.where(has_after, me + 2, me - 2)
+    at_inlet = me < 2
+    after_inlet = (me >= 2) & (me < 4)
+
+    barrier = pltpu.get_barrier_semaphore()
+    pl.semaphore_signal(barrier, inc=1, device_id={"gx": partner}, device_id_type=MESH)
+
+    @pl.when(has_after)
+    def _():
+        pl.semaphore_signal(barrier, inc=1, device_id={"gx": after}, device_id_type=MESH)
+
+    @pl.when(has_before)
+    def _():
+        pl.semaphore_signal(barrier, inc=1, device_id={"gx": me - 2}, device_id_type=MESH)
+
+    pl.semaphore_wait(barrier, 1 + has_after.astype(jnp.int32) + has_before.astype(jnp.int32))
+
+    def block_rows(block):
+        return pl.ds(pl.multiple_of(block * STRIDE, STRIDE), STRIDE)
+
+    def far_copy(source, block):
+        return pltpu.make_async_remote_copy(
+            src_ref=source.at[:, block_rows(block), :],
+            dst_ref=far.at[:, block_rows(block), :],
+            send_sem=far_send.at[block],
+            recv_sem=far_recv.at[block],
+            device_id={"gx": after},
+            device_id_type=MESH,
+        )
+
+    def back_copy(block):
+        return pltpu.make_async_remote_copy(
+            src_ref=back.at[:, block_rows(block), :],
+            dst_ref=theirs_ref.at[:, block_rows(block), :],
+            send_sem=back_send.at[block],
+            recv_sem=back_recv.at[block],
+            device_id={"gx": partner},
+            device_id_type=MESH,
+        )
+
+    @pl.when(has_after & even)
+    def _():
+        @pl.loop(0, blocks)
+        def _(block):
+            far_copy(next_ref, block).start()
+
+    @pl.when(has_after & (me % 2 == 1))
+    def _():
+        @pl.loop(0, blocks)
+        def _(block):
+            far_copy(near_ref, block).start()
+
+    @pl.when(me < 2)
+    def _():
+        far[...] = jnp.zeros_like(far)
+
+    @pl.when(has_before)
+    def _():
+        far_copy(near_ref, 0).wait_recv()
+
     local = lax.broadcasted_iota(jnp.int32, (WINDOW, LANES), 0)
 
-    def window(index, carry):
-        start = pl.multiple_of(jnp.minimum(index * stride, rows - WINDOW), HALO)
+    @pl.loop(0, blocks)
+    def _(block):
+        @pl.when(has_before & (block + 1 < blocks))
+        def _():
+            far_copy(near_ref, block + 1).wait_recv()
+
+        start = pl.multiple_of(jnp.clip(block * STRIDE - HALO, 0, rows - WINDOW), HALO)
         here = pl.ds(start, WINDOW)
-        low_wall = local + start == 0
-        high_wall = local + start == rows - 1
-        mean = mean_ref[here, :]
-        drag = mean + 2.0 * viscosity
-
-        def load(ref):
-            return [ref[c, here, :].astype(jnp.float32) for c in range(3)]
-
-        def rate(field, behind):
-            half = 0.5 * field[1]
-            up, down = viscosity - half, viscosity + half
-            out = []
-            for c in range(3):
-                above = jnp.where(high_wall, 0.0, jnp.roll(field[c], -1, axis=0))
-                below = jnp.where(low_wall, 0.0, jnp.roll(field[c], 1, axis=0))
-                out.append(up * above + down * below + mean * behind[c] - drag * field[c])
-            return out
-
-        def pick(flag, first, second):
-            return [jnp.where(flag, a, b) for a, b in zip(first, second)]
-
-        def rounded(field):
-            return [a.astype(jnp.bfloat16).astype(jnp.float32) for a in field]
-
-        def one(field, f0):
-            return [u + time_step * (8.0 / 15.0) * a for u, a in zip(field, f0)]
-
-        def two(field, f1, f0):
-            return [
-                u + (time_step * 5.0 / 12.0) * b - (time_step * 17.0 / 60.0) * a
-                for u, b, a in zip(field, f1, f0)
-            ]
-
-        def three(field, f2, f1):
-            return [
-                u + (time_step * 0.75) * b - (time_step * 5.0 / 12.0) * a
-                for u, b, a in zip(field, f2, f1)
-            ]
-
-        inlet = load(inlet_ref)
-        far = pick(after_inlet, inlet, load(far_ref))
-        q0, q1, p0, p1 = load(q0_ref), load(q1_ref), load(p0_ref), load(p1_ref)
-        q0_1 = rounded(one(q0, rate(q0, far)))
-        q1_f0 = rate(q1, q0)
-        q1_1 = one(q1, q1_f0)
-        q1_2 = rounded(two(q1_1, rate(q1_1, q0_1), q1_f0))
-        p0_f0 = rate(p0, pick(at_inlet, inlet, q1))
-        p0_1 = one(p0, p0_f0)
-        p0_f1 = rate(p0_1, pick(at_inlet, inlet, rounded(q1_1)))
-        p0_2 = two(p0_1, p0_f1, p0_f0)
-        p0_3 = three(p0_2, rate(p0_2, pick(at_inlet, inlet, q1_2)), p0_f1)
-        p1_f0 = rate(p1, p0)
-        p1_1 = one(p1, p1_f0)
-        p1_f1 = rate(p1_1, rounded(p0_1))
-        p1_2 = two(p1_1, p1_f1, p1_f0)
-        p1_3 = three(p1_2, rate(p1_2, rounded(p0_2)), p1_f1)
-        inner = pl.ds(pl.multiple_of(start + HALO, HALO), WINDOW - HALO)
-        results = ((o0_ref, p0_3), (o1_ref, p1_3))
-        for ref, value in results:
-            for c in range(3):
-                ref[c, inner, :] = value[c][HALO:].astype(ref.dtype)
-
-        @pl.when(index == 0)
-        def _():
-            for ref, value in results:
+
+        @pl.loop(0, keep_ref.shape[2] // LANES)
+        def _(column):
+            lanes = pl.ds(pl.multiple_of(column * LANES, LANES), LANES)
+            low_wall = local + start == 0
+            high_wall = local + start == rows - 1
+            mean = mean_ref[here, :]
+            drag = mean + 2.0 * viscosity
+
+            def load(ref):
+                return [ref[c, here, lanes].astype(jnp.float32) for c in range(3)]
+
+            def rate(field, behind):
+                half = 0.5 * field[1]
+                up, down = viscosity - half, viscosity + half
+                out = []
                 for c in range(3):
-                    ref[c, 0:HALO, :] = value[c][:HALO].astype(ref.dtype)
-
-        return carry
-
-    lax.fori_loop(0, count, window, 0)
-
-
-def march(level, mean_lanes, inlet, far, q0, q1, p0, p1):
-    shape = p0.shape
+                    above = jnp.where(high_wall, 0.0, jnp.roll(field[c], -1, axis=0))
+                    below = jnp.where(low_wall, 0.0, jnp.roll(field[c], 1, axis=0))
+                    out.append(up * above + down * below + mean * behind[c] - drag * field[c])
+                return out
+
+            def pick(flag, first, second):
+                return [jnp.where(flag, a, b) for a, b in zip(first, second)]
+
+            def rounded(field):
+                return [a.astype(jnp.bfloat16).astype(jnp.float32) for a in field]
+
+            def one(field, f0):
+                return [u + time_step * (8.0 / 15.0) * a for u, a in zip(field, f0)]
+
+            def two(field, f1, f0):
+                return [
+                    u + (time_step * 5.0 / 12.0) * b - (time_step * 17.0 / 60.0) * a
+                    for u, b, a in zip(field, f1, f0)
+                ]
+
+            def three(field, f2, f1):
+                return [
+                    u + (time_step * 0.75) * b - (time_step * 5.0 / 12.0) * a
+                    for u, b, a in zip(field, f2, f1)
+                ]
+
+            inlet = load(inlet_ref)
+            keep, other, near, further = load(keep_ref), load(other_ref), load(near_ref), load(next_ref)
+            p0, p1 = pick(even, keep, other), pick(even, other, keep)
+            q0, q1 = pick(even, near, further), pick(even, further, near)
+            q0_1 = rounded(one(q0, rate(q0, pick(after_inlet, inlet, load(far)))))
+            q1_f0 = rate(q1, q0)
+            q1_1 = one(q1, q1_f0)
+            q1_2 = rounded(two(q1_1, rate(q1_1, q0_1), q1_f0))
+            p0_f0 = rate(p0, pick(at_inlet, inlet, q1))
+            p0_1 = one(p0, p0_f0)
+            p0_f1 = rate(p0_1, pick(at_inlet, inlet, rounded(q1_1)))
+            p0_2 = two(p0_1, p0_f1, p0_f0)
+            p0_3 = three(p0_2, rate(p0_2, pick(at_inlet, inlet, q1_2)), p0_f1)
+            p1_f0 = rate(p1, p0)
+            p1_1 = one(p1, p1_f0)
+            p1_f1 = rate(p1_1, rounded(p0_1))
+            p1_2 = two(p1_1, p1_f1, p1_f0)
+            p1_3 = three(p1_2, rate(p1_2, rounded(p0_2)), p1_f1)
+            results = ((mine_ref, pick(even, p0_3, p1_3)), (back, pick(even, p1_3, p0_3)))
+
+            def store(skip):
+                for ref, value in results:
+                    for c in range(3):
+                        ref[c, block_rows(block), lanes] = value[c][skip : skip + STRIDE].astype(ref.dtype)
+
+            pl.when(block == 0)(lambda: store(0))
+            pl.when((block > 0) & (block < blocks - 1))(lambda: store(HALO))
+            pl.when(block == blocks - 1)(lambda: store(2 * HALO))
+
+        back_copy(block).start()
+
+    @pl.loop(0, blocks)
+    def _(block):
+        back_copy(block).wait_send()
+        back_copy(block).wait_recv()
+
+    @pl.when(has_after)
+    def _():
+        @pl.loop(0, blocks)
+        def _(block):
+            far_copy(near_ref, block).wait_send()
+
+
+def march(slabs, mean_lanes, inlet, keep, other, near, next_near):
+    shape = keep.shape
     rows = shape[1]
-    flops = 9 * 3 * 12 * rows * LANES
+    blocks = rows // STRIDE
+    vmem = pl.BlockSpec(memory_space=pltpu.VMEM)
     return pl.pallas_call(
-        march_kernel,
+        functools.partial(march_kernel, slabs),
         out_shape=[jax.ShapeDtypeStruct(shape, jnp.bfloat16)] * 2,
-        in_specs=[pl.BlockSpec(memory_space=pltpu.SMEM)] + [pl.BlockSpec(memory_space=pltpu.VMEM)] * 7,
-        out_specs=[pl.BlockSpec(memory_space=pltpu.VMEM)] * 2,
-        compiler_params=pltpu.CompilerParams(vmem_limit_bytes=28 * 1024 * 1024),
-        cost_estimate=pl.CostEstimate(flops=flops, bytes_accessed=16 * 3 * rows * LANES, transcendentals=0),
+        in_specs=[vmem] * 6,
+        out_specs=[vmem, pl.BlockSpec(memory_space=pl.ANY)],
+        scratch_shapes=[
+            pltpu.VMEM(shape, jnp.bfloat16),
+            pltpu.VMEM(shape, jnp.bfloat16),
+            pltpu.SemaphoreType.DMA((blocks,)),
+            pltpu.SemaphoreType.DMA((blocks,)),
+            pltpu.SemaphoreType.DMA((blocks,)),
+            pltpu.SemaphoreType.DMA((blocks,)),
+        ],
+        compiler_params=pltpu.CompilerParams(
+            collective_id=0, has_side_effects=True, vmem_limit_bytes=36 * 1024 * 1024
+        ),
+        cost_estimate=pl.CostEstimate(
+            flops=324 * math.prod(shape), bytes_accessed=14 * math.prod(shape), transcendentals=0
+        ),
         name="march",
-    )(level, mean_lanes, inlet, far, q0, q1, p0, p1)
+    )(mean_lanes, inlet, keep, other, near, next_near)
 
 
 def inlet_planes(mean_flow, chol_diag, chol_off, eddy_x, eddy_y, eddy_z, eddy_signs, columns, spanwise, held, forward):
@@ -306,29 +406,12 @@
     inflow, (other, near), next_near = inlet_planes(
         mean_flow, chol_diag, chol_off, eddy_x, eddy_y, eddy_z, eddy_signs, columns, spanwise, (other, near), forward
     )
-    inflow, next_near = lax.optimization_barrier((inflow, next_near))
-    p0 = jnp.where(even, keep, other)
-    p1 = jnp.where(even, other, keep)
-    q0 = jnp.where(even, near, next_near)
-    q1 = jnp.where(even, next_near, near)
-    chunks = []
-    for begin in range(0, half, LANES):
-        cut = [value[:, :, begin : begin + LANES] for value in (q0, q1, p0, p1)]
-        chunks.append((lax.ppermute(cut[1], "gx", onward), *cut))
+    inlet = jnp.where(even, inflow[:, :, :half], inflow[:, :, half:]).astype(jnp.bfloat16)
     mean_lanes = jnp.broadcast_to(mean_flow[:, None], (rows, LANES))
-    level = (me // 2).astype(jnp.int32).reshape(1)
-    lows, highs = [], []
-    for number, planes in enumerate(chunks):
-        begin = number * LANES
-        inlet = jnp.where(
-            even, inflow[:, :, begin : begin + LANES], inflow[:, :, half + begin : half + begin + LANES]
-        ).astype(jnp.bfloat16)
-        o0, o1 = march(level, mean_lanes, inlet, *planes)
-        keep = jnp.where(even, o0, o1)
-        other = lax.ppermute(jnp.where(even, o1, o0), "gx", swap)
-        lows.append(jnp.where(even, keep, other))
-        highs.append(jnp.where(even, other, keep))
-    velocity_next = jnp.concatenate(lows + highs, axis=2)[:, None]
+    mine, theirs = march(slabs, mean_lanes, inlet, keep, other, near, next_near)
+    velocity_next = jnp.concatenate(
+        [jnp.where(even, mine, theirs), jnp.where(even, theirs, mine)], axis=2
+    )[:, None]
     return (velocity_next, inflow[None])
 
 

time: 169 us -> 150 us (0.89)
  waiting for transfers between devices: 53.2 us -> 18.6 us
  Pallas kernels: 30.2 us -> 54.9 us
  starting transfers between devices: 16.9 us -> 8.58 us
  other arithmetic: 32.4 us -> 26 us
  matrix products: 18.3 us -> 22.2 us
  local copies, waits for them, and re-layouts: 6.28 us -> 8.85 us
    ppermute x4 -> x0, waiting for transfers between devices: 32 us -> none  [the longest x2 17.2 us: body(): other = lax.ppermute(jnp.where(even, o1, o0), 'gx', swap)]
    pallas_call x2 -> x1, Pallas kernels: 27.5 us -> 52.2 us  [march(): pl.pallas_call(functools.partial(march_kernel, slabs), out_shape=[jax.Sha...]
    ppermute x4 -> x0, starting transfers between devices: 8.46 us -> none  [the longest x2 6.97 us: body(): chunks.append((lax.ppermute(cut[1], 'gx', onward), *cut))]
    select_n x6 -> x2, other arithmetic: 6.95 us -> 0.22 us  [the longest x1 0.21 us: body(): jnp.where(even, mine, theirs)]
    broadcast_in_dim x0 -> x1, other arithmetic: none -> 3.41 us  [body(): return (velocity_next, inflow[None])]
    unnamed x65 -> x72, local copies, waits for them, and re-layouts: 4.57 us -> 7.59 us
    ppermute x1, waiting for transfers between devices: 20.7 us -> 17.9 us  [forward(): return lax.ppermute(held[0], 'gx', onward)]
    select_n x1, other arithmetic: 3.07 us -> 0.35 us  [wall_bases(): jnp.where(jnp.arange(rows)[:, None] == 0, math.sqrt(1.0 / rows), cosine)]
  transfers between devices with their start and end apart: 7 -> 3, of which waited for: 6 -> 2; matrix products, arithmetic and copies ran while one was open for 25% -> 26% of each run, Pallas kernels for 18% -> 0%
where the time goes in v1:
time: 150 us
  Pallas kernels  54.9 us (37%)
  other arithmetic  26 us (17%)
  matrix products  22.2 us (15%)
  waiting for transfers between devices  18.6 us (12%)
  local copies, waits for them, and re-layouts  8.85 us (6%)
  starting transfers between devices  8.58 us (6%)
  between operations  5.23 us (3%)
  blocking collectives  5.19 us (3%)
    pallas_call x1, Pallas kernels, march(): pl.pallas_call(functools.partial(march_kernel, slabs), out_shape=[jax.Sha...  52.2 us
    ppermute x1, waiting for transfers between devices, forward(): return lax.ppermute(held[0], 'gx', onward)  17.9 us
    dot_general x2, matrix products, fluct_at(): jnp.einsum('ey,jez->jyz', shape_y, weight, preferred_element_type=jnp.flo...  10.6 us
    dot_general x1, matrix products, inlet_planes(): modes = jnp.einsum('yz,ky->zk', div, cosine, precision=high)  9.04 us
    unnamed x72, local copies, waits for them, and re-layouts  7.59 us
    all_gather x1, blocking collectives, line_solve(): everyone = lax.all_gather(sums, axis)  5.19 us
    ppermute x1, starting transfers between devices, forward(): return lax.ppermute(held[0], 'gx', onward)  3.62 us
    mul x1, other arithmetic, inlet_planes(): flux = second * (cells_y < rows - 1).astype(jnp.float32)[:, None]  3.59 us
  transfers between devices with their start and end apart: 3, of which 2 were waited for; matrix products, arithmetic and copies ran while one was open for 26% of the time, Pallas kernels for 0%

profile of v1, /device:TPU:8, one launch (start us, length us, event | category | flops | bytes accessed | tf_op | source)
XLA Modules:
  0.0 149.6 jit_solution(3520708049376740970)
XLA Ops:
  0.7 3.3 %broadcast_select_fusion.2 = (bf16[3,1024,256]{2,1,0:T(8,128)(2,1)S(1)}, bf16[3,1024,256]{2,1,0:T(8,128)(2,1)}) fusion(pred[]{:T(512)S(6)} %eq.52, bf16[3,1024,512]{2,1,0:T(8,128)(2,1)} %bitcast.103), kind=kLoop, calls=%fused_computation.50 | loop fusion | flops 1572864 | bytes 6291457 | tf_op jit(solution)/shard_map/jit(_where)/select_n | solution.py:399
  4.0 1.5 collective-permute-start
  5.5 3.5 %collective-permute-start.1 = (bf16[3,1024,256]{2,1,0:T(8,128)(2,1)S(1)}, bf16[3,1024,256]{2,1,0:T(8,128)(2,1)S(1)}, u32[]{:S(2)}, u32[]{:S(2)}) collective-permute-start(bf16[3,1024,256]{2,1,0:T(8,128)(2,1)S(1)} %get-tuple-element.47.keep_ref), channel_id=1, source_target_pairs={{0,8},{4,12},{8,16},{12,20},{16,24},{20,28},{1,9},{5,13},{9,17},{1... | collective-permute-start | bytes 4718600 | tf_op jit(solution)/shard_map/ppermute | solution.py:401
  9.1 2.1 %fusion.10 = f32[1536,512]{0,1:T(8,128)S(1)} fusion(s32[1536]{0:T(1024)S(1)} %copy-done.25, s32[512]{0:T(512)S(1)} %iota_add_fusion), kind=kLoop, calls=%fused_computation.20 | loop fusion | flops 15728640 | bytes 3153920 | tf_op jit(solution)/shard_map/mul | solution.py:28
  11.3 1.8 %fusion.13 = f32[3,1024]{1,0:T(4,128)S(1)} fusion(s32[1536]{0:T(1024)S(1)} %copy-done.34, f32[3,1536]{1,0:T(4,128)S(1)} %convert_multiply_fusion, f32[1536]{0:T(1024)S(1)} %fusion.43), kind=kOutput, calls=%fused_computation.25 | convolution fusion | flops 22029312 | bytes 43008 | tf_op jit(solution)/shard_map/ey,jez->jyz/dot_general | solution.py:360
  13.1 8.8 %fusion.14 = f32[3,1024,512]{2,1,0:T(8,128)} fusion(s32[1536]{0:T(1024)S(1)} %copy-done.34, f32[1536,512]{0,1:T(8,128)S(1)} %fusion.10, f32[3,1536]{1,0:T(4,128)S(1)} %convert_multiply_fusion), kind=kOutput, calls=%fused_computation.26 | convolution fusion | flops 4849139712 | bytes 9461760 | tf_op jit(solution)/shard_map/ey,jez->jyz/dot_general | solution.py:360
  21.9 1.0 copy.41
  23.0 3.6 %fusion.23 = (f32[1024,512]{1,0:T(8,128)S(1)}, f32[1024,512]{1,0:T(8,128)S(1)}) fusion(f32[3,1024,512]{2,1,0:T(8,128)} %fusion.14, f32[1024]{0:T(1024)S(1)} %fusion.46, f32[1024]{0:T(1024)S(1)} %bitcast.113, f32[1024]{0:T(1024)S(1)} %bitcast.109, f32[1024]{0:T(1024)S(1)} %bitcast.112, f32[1024]{0:T(1024)S(1)} %bitcast.110, f32[1024]{0:T(1024)S(1)} %bitcast.111), kind=kLoop, calls=%fused_computation.38 | loop fusion | flops 4718592 | bytes 10510336 | tf_op jit(solution)/shard_map/mul | solution.py:371
  26.6 2.4 %multiply_subtract_fusion = (f32[32,32,1024]{2,1,0:T(8,128)S(1)}, bf16[32,32,1024]{2,1,0:T(8,128)(2,1)}) fusion(f32[32,1024]{1,0:T(8,128)S(1)} %copy-done.18, f32[32,1024]{1,0:T(8,128)S(1)} %copy-done.19, f32[32,1024]{1,0:T(8,128)S(1)} %copy-done.20, f32[32,1024]{1,0:T(8,128)S(1)} %copy-done.21, pred[32,32]{1,0:T(8,128)(4,1)S(1)} %add_compare_fusion), kind=kLoop, calls=%fused_computation.11 | loop fusion | flops 5242880 | bytes 6816768 | tf_op jit(solution)/shard_map/sub | solution.py:46
  29.5 0.7 copy-done.11
  30.2 9.0 %multiply_reduce_fusion = (f32[16,1024]{1,0:T(8,128)S(1)}, f32[16,1024]{1,0:T(8,128)S(1)}, f32[512,1024]{1,0:T(8,128)}) fusion(f32[32,1024]{1,0:T(8,128)S(1)} %copy-done.12, f32[32,1024]{1,0:T(8,128)S(1)} %copy-done.13, f32[1024,1024]{1,0:T(8,128)S(1)} %bitcast_select_fusion, f32[1024,511]{1,0:T(8,128)S(1)} %bitcast.100, f32[1024,1]{1,0:T(8,128)S(1)} %copy-done.11, ...), kind=kOutput, calls=%fused_computation.42 | convolution fusion | flops 3225387008 | bytes 15071232 | tf_op jit(solution)/shard_map/yz,ky->zk/dot_general | solution.py:377
  39.2 3.3 %multiply_add_fusion = f32[1,1024,512]{2,1,0:T(8,128)} fusion(f32[3,1024,512]{2,1,0:T(8,128)} %fusion.14, f32[1024]{0:T(1024)S(1)} %bitcast.118, f32[1024]{0:T(1024)S(1)} %copy-done.28), kind=kLoop, calls=%fused_computation.47 | loop fusion | flops 1048576 | bytes 4202496 | tf_op jit(solution)/shard_map/add | solution.py:368
  42.6 0.7 collective-permute-done.1.near_ref
  43.3 3.6 %collective-permute-start.2 = (bf16[3,1024,256]{2,1,0:T(8,128)(2,1)}, bf16[3,1024,256]{2,1,0:T(8,128)(2,1)}, u32[]{:S(2)}, u32[]{:S(2)}) collective-permute-start(bf16[3,1024,256]{2,1,0:T(8,128)(2,1)} %collective-permute-done.other_ref), channel_id=1, source_target_pairs={{0,8},{4,12},{8,16},{12,20},{16,24},{20,28},{1,9},{5,13},{9,17},{1... | collective-permute-start | bytes 4718600 | tf_op jit(solution)/shard_map/ppermute | solution.py:404
  46.9 2.0 %add_convert_fusion = bf16[32,32,1024]{2,1,0:T(8,128)(2,1)} fusion(f32[32,1024]{1,0:T(8,128)S(1)} %copy-done.14, f32[32,1024]{1,0:T(8,128)S(1)} %copy-done.15, f32[32,1024]{1,0:T(8,128)S(1)} %copy-done.16, f32[32,1024]{1,0:T(8,128)S(1)} %copy-done.17), kind=kLoop, calls=%fused_computation.12 | loop fusion | flops 4194304 | bytes 2621440 | tf_op jit(solution)/shard_map/convert_element_type | solution.py:383
  48.9 2.1 %copy.47 = f32[64,8,8,128]{3,2,1,0:T(8,128)S(1)} copy(f32[64,8,8,128]{3,1,2,0:T(8,128)} %bitcast.102) | data formatting | bytes 4194304
  51.1 5.2 %all-gather.1 = f32[4,2,1024]{2,1,0:T(2,128)S(1)} all-gather(f32[1,2,1024]{2,1,0:T(2,128)S(1)} %maximum_bitcast_fusion.1), channel_id=2, replica_groups=mesh['gx'=8,'yz'=4] {'yz'}, dimensions={0}, use_global_device_ids=true | all-gather | bytes 40960 | tf_op jit(solution)/shard_map/all_gather | solution.py:112
  56.3 0.6 slice_reduce_fusion
  58.6 0.6 fusion.48
  59.3 0.7 fusion.55
  62.6 17.9 %collective-permute-done.2.next_ref = bf16[3,1024,256]{2,1,0:T(8,128)(2,1)} collective-permute-done((bf16[3,1024,256]{2,1,0:T(8,128)(2,1)}, bf16[3,1024,256]{2,1,0:T(8,128)(2,1)}, u32[]{:S(2)}, u32[]{:S(2)}) %collective-permute-start.2) | collective-permute-done | bytes 1572896 | tf_op jit(solution)/shard_map/ppermute | solution.py:404
  80.6 2.7 %line_solve.1 = (f32[512,8,128]{2,1,0:T(8,128)S(1)}, f32[512,8,128]{2,1,0:T(8,128)S(1)}) custom-call(f32[512,8,128]{2,1,0:T(8,128)S(1)} %bitcast.98, f32[6,8,128]{2,1,0:T(8,128)S(1)} %bitcast.99), custom_call_target="tpu_custom_call" | custom-call | flops 5242880 | bytes 6291456 | tf_op jit(solution)/shard_map/line_solve/pallas_call | solution.py:137
  83.5 1.3 copy-done.8
  84.8 0.6 copy-done.10
  85.5 1.3 subtract_bitcast_fusion.1
  87.1 0.6 copy-done.9
  87.7 1.3 subtract_bitcast_fusion
  89.3 0.7 pad_maximum_fusion
  89.9 3.4 %fusion.66 = f32[1,3,1024,512]{3,2,1,0:T(8,128)} fusion(f32[1,1024,512]{2,1,0:T(8,128)S(1)} %subtract_bitcast_fusion, f32[1,1024,512]{2,1,0:T(8,128)S(1)} %subtract_bitcast_fusion.1, f32[1,1024,512]{2,1,0:T(8,128)S(1)} %copy-done.4), kind=kLoop, calls=%fused_computation.125 | loop fusion | flops 3145728 | bytes 12582912 | tf_op jit(solution)/shard_map/broadcast_in_dim | solution.py:415
  93.7 1.0 copy-done.1
  95.2 52.2 %march.1 = (bf16[3,1024,256]{2,1,0:T(8,128)(2,1)S(1)}, bf16[3,1024,256]{2,1,0:T(8,128)(2,1)S(1)}) custom-call(f32[1024,128]{1,0:T(8,128)S(1)} %broadcast_in_dim.34.mean_ref, bf16[3,1024,256]{2,1,0:T(8,128)(2,1)S(1)} %fusion.11.inlet_ref, bf16[3,1024,256]{2,1,0:T(8,128)(2,1)S(1)} %copy-done.1, bf16[3,1024,256]{2,1,0:T(8,128)(2,1)} %collective-permute-done.other_ref, ...), custom_call_target="tpu_custom_call" | custom-call | flops 254803968 | bytes 11010048 | tf_op jit(solution)/shard_map/march/pallas_call | solution.py:324
  147.7 1.9 %maximum_bitcast_fusion = bf16[3,1,1024,512]{3,2,1,0:T(8,128)(2,1)} fusion(bf16[3,1024,256]{2,1,0:T(8,128)(2,1)S(1)} %get-tuple-element.46, bf16[3,1024,256]{2,1,0:T(8,128)(2,1)S(1)} %get-tuple-element.45), kind=kLoop, calls=%fused_computation.23 | loop fusion | flops 6291456 | bytes 6291456
  (90 shorter events, 2.8 us)
Async XLA Ops:
  0.6 8.4 %copy-start.31 = (s32[1536]{0:T(1024)S(1)}, s32[1536]{0:T(1024)}, u32[]{:S(2)}) copy-start(s32[1536]{0:T(1024)} %param.29) | copy-start | bytes 18436
  0.7 8.4 %copy-start.25 = (s32[1536]{0:T(1024)S(1)}, s32[1536]{0:T(1024)}, u32[]{:S(2)}) copy-start(s32[1536]{0:T(1024)} %param.31) | copy-start | bytes 18436
  4.0 9.1 %copy-start = (bf16[3,1024,256]{2,1,0:T(8,128)(2,1)}, bf16[3,1024,256]{2,1,0:T(8,128)(2,1)S(1)}, u32[]{:S(2)}) copy-start(bf16[3,1024,256]{2,1,0:T(8,128)(2,1)S(1)} %get-tuple-element.47.keep_ref) | copy-start | bytes 4718596
  4.0 7.2 %copy-start.26 = (s32[3,1536]{1,0:T(4,128)S(1)}, s32[3,1536]{1,0:T(4,128)}, u32[]{:S(2)}) copy-start(s32[3,1536]{1,0:T(4,128)} %param.32) | copy-start | bytes 55300
  4.0 7.3 %copy-start.34 = (s32[1536]{0:T(1024)S(1)}, s32[1536]{0:T(1024)}, u32[]{:S(2)}) copy-start(s32[1536]{0:T(1024)} %param.30) | copy-start | bytes 18436
  4.0 38.6 %collective-permute-start = (bf16[3,1024,256]{2,1,0:T(8,128)(2,1)}, bf16[3,1024,256]{2,1,0:T(8,128)(2,1)}, u32[]{:S(2)}, u32[]{:S(2)}) collective-permute-start(bf16[3,1024,256]{2,1,0:T(8,128)(2,1)} %get-tuple-element.48), channel_id=1, source_target_pairs={{0,4},{4,0},{8,12},{12,8},{16,20},{20,16},{24,28},{28,24},{1,5},{5... | collective-permute-start | bytes 4718600 | tf_op jit(solution)/shard_map/ppermute | solution.py:400
  5.5 37.7 %collective-permute-start.1 = (bf16[3,1024,256]{2,1,0:T(8,128)(2,1)S(1)}, bf16[3,1024,256]{2,1,0:T(8,128)(2,1)S(1)}, u32[]{:S(2)}, u32[]{:S(2)}) collective-permute-start(bf16[3,1024,256]{2,1,0:T(8,128)(2,1)S(1)} %get-tuple-element.47.keep_ref), channel_id=1, source_target_pairs={{0,8},{4,12},{8,16},{12,20},{16,24},{20,28},{1,9},{5,13},{9,17},{1... | collective-permute-start | bytes 4718600 | tf_op jit(solution)/shard_map/ppermute | solution.py:401
  13.1 8.8 %copy-start.29 = (f32[3,1024]{1,0:T(4,128)S(1)}, f32[3,1024]{1,0:T(4,128)}, u32[]{:S(2)}) copy-start(f32[3,1024]{1,0:T(4,128)} %param.27) | copy-start | bytes 36868
  13.1 8.8 %copy-start.30 = (f32[3,1024]{1,0:T(4,128)S(1)}, f32[3,1024]{1,0:T(4,128)}, u32[]{:S(2)}) copy-start(f32[3,1024]{1,0:T(4,128)} %param.28) | copy-start | bytes 36868
  23.0 3.6 %copy-start.18 = (f32[32,1024]{1,0:T(8,128)S(1)}, f32[32,1024]{1,0:T(8,128)}, u32[]{:S(2)}) copy-start(f32[32,1024]{1,0:T(8,128)} %constant.174.clone) | copy-start | bytes 393220
  23.0 3.6 %copy-start.19 = (f32[32,1024]{1,0:T(8,128)S(1)}, f32[32,1024]{1,0:T(8,128)}, u32[]{:S(2)}) copy-start(f32[32,1024]{1,0:T(8,128)} %constant.173.clone) | copy-start | bytes 393220
  23.0 3.6 %copy-start.20 = (f32[32,1024]{1,0:T(8,128)S(1)}, f32[32,1024]{1,0:T(8,128)}, u32[]{:S(2)}) copy-start(f32[32,1024]{1,0:T(8,128)} %constant.172.clone) | copy-start | bytes 393220
  23.0 3.6 %copy-start.21 = (f32[32,1024]{1,0:T(8,128)S(1)}, f32[32,1024]{1,0:T(8,128)}, u32[]{:S(2)}) copy-start(f32[32,1024]{1,0:T(8,128)} %constant.171.clone) | copy-start | bytes 393220
  26.6 2.8 %copy-start.5 = (f32[1024,512]{1,0:T(8,128)}, f32[1024,512]{1,0:T(8,128)S(1)}, u32[]{:S(2)}) copy-start(f32[1024,512]{1,0:T(8,128)S(1)} %get-tuple-element.44) | copy-start | bytes 6291460
  26.6 2.8 %copy-start.7 = (f32[1024,512]{1,0:T(8,128)}, f32[1024,512]{1,0:T(8,128)S(1)}, u32[]{:S(2)}) copy-start(f32[1024,512]{1,0:T(8,128)S(1)} %get-tuple-element.43) | copy-start | bytes 6291460
  30.2 9.1 %copy-start.28 = (f32[1024]{0:T(1024)S(1)}, f32[1024]{0:T(1024)}, u32[]{:S(2)}) copy-start(f32[1024]{0:T(1024)} %param.26) | copy-start | bytes 12292
  39.2 7.7 %copy-start.14 = (f32[32,1024]{1,0:T(8,128)S(1)}, f32[32,1024]{1,0:T(8,128)}, u32[]{:S(2)}) copy-start(f32[32,1024]{1,0:T(8,128)} %constant.178.clone) | copy-start | bytes 393220
  39.2 7.7 %copy-start.15 = (f32[32,1024]{1,0:T(8,128)S(1)}, f32[32,1024]{1,0:T(8,128)}, u32[]{:S(2)}) copy-start(f32[32,1024]{1,0:T(8,128)} %constant.177.clone) | copy-start | bytes 393220
  39.2 7.7 %copy-start.16 = (f32[32,1024]{1,0:T(8,128)S(1)}, f32[32,1024]{1,0:T(8,128)}, u32[]{:S(2)}) copy-start(f32[32,1024]{1,0:T(8,128)} %constant.176.clone) | copy-start | bytes 393220
  39.2 7.7 %copy-start.17 = (f32[32,1024]{1,0:T(8,128)S(1)}, f32[32,1024]{1,0:T(8,128)}, u32[]{:S(2)}) copy-start(f32[32,1024]{1,0:T(8,128)} %constant.175.clone) | copy-start | bytes 393220
  43.2 5.7 %copy-start.2 = (bf16[3,1024,256]{2,1,0:T(8,128)(2,1)}, bf16[3,1024,256]{2,1,0:T(8,128)(2,1)S(1)}, u32[]{:S(2)}) copy-start(bf16[3,1024,256]{2,1,0:T(8,128)(2,1)S(1)} %collective-permute-done.1.near_ref) | copy-start | bytes 4718596
  43.2 7.8 %copy-start.22 = (f32[16,1024]{1,0:T(8,128)S(1)}, f32[16,1024]{1,0:T(8,128)}, u32[]{:S(2)}) copy-start(f32[16,1024]{1,0:T(8,128)} %constant.183.clone) | copy-start | bytes 196612
  43.2 7.8 %copy-start.23 = (f32[16,1024]{1,0:T(8,128)S(1)}, f32[16,1024]{1,0:T(8,128)}, u32[]{:S(2)}) copy-start(f32[16,1024]{1,0:T(8,128)} %constant.182.clone) | copy-start | bytes 196612
  43.2 7.8 %copy-start.24 = (f32[16,1024]{1,0:T(8,128)S(1)}, f32[16,1024]{1,0:T(8,128)}, u32[]{:S(2)}) copy-start(f32[16,1024]{1,0:T(8,128)} %constant.181.clone) | copy-start | bytes 196612
  43.2 19.2 %copy-start.32 = (f32[1024]{0:T(1024)S(1)}, f32[1024]{0:T(1024)}, u32[]{:S(2)}) copy-start(f32[1024]{0:T(1024)} %constant.190) | copy-start | bytes 12292
  43.3 19.3 %copy-start.33 = (f32[1024]{0:T(1024)S(1)}, f32[1024]{0:T(1024)}, u32[]{:S(2)}) copy-start(f32[1024]{0:T(1024)} %constant.185.clone) | copy-start | bytes 12292
  43.3 19.3 %copy-start.27 = (f32[3,1024]{1,0:T(4,128)S(1)}, f32[3,1024]{1,0:T(4,128)}, u32[]{:S(2)}) copy-start(f32[3,1024]{1,0:T(4,128)} %constant.186.clone) | copy-start | bytes 36868
  43.3 37.3 %collective-permute-start.2 = (bf16[3,1024,256]{2,1,0:T(8,128)(2,1)}, bf16[3,1024,256]{2,1,0:T(8,128)(2,1)}, u32[]{:S(2)}, u32[]{:S(2)}) collective-permute-start(bf16[3,1024,256]{2,1,0:T(8,128)(2,1)} %collective-permute-done.other_ref), channel_id=1, source_target_pairs={{0,8},{4,12},{8,16},{12,20},{16,24},{20,28},{1,9},{5,13},{9,17},{1... | collective-permute-start | bytes 4718600 | tf_op jit(solution)/shard_map/ppermute | solution.py:404
  83.3 1.6 %copy-start.8 = (f32[1024,512]{1,0:T(8,128)S(1)}, f32[1024,512]{1,0:T(8,128)}, u32[]{:S(2)}) copy-start(f32[1024,512]{1,0:T(8,128)} %copy-done.7) | copy-start | bytes 6291460
  83.3 2.2 %copy-start.10 = (bf16[32,32,1024]{2,1,0:T(8,128)(2,1)S(1)}, bf16[32,32,1024]{2,1,0:T(8,128)(2,1)}, u32[]{:S(2)}) copy-start(bf16[32,32,1024]{2,1,0:T(8,128)(2,1)} %add_convert_fusion) | copy-start | bytes 6291460
  85.5 2.2 %copy-start.9 = (bf16[32,32,1024]{2,1,0:T(8,128)(2,1)S(1)}, bf16[32,32,1024]{2,1,0:T(8,128)(2,1)}, u32[]{:S(2)}) copy-start(bf16[32,32,1024]{2,1,0:T(8,128)(2,1)} %get-tuple-element.50) | copy-start | bytes 6291460
  93.4 1.9 %copy-start.3 = (bf16[3,1024,256]{2,1,0:T(8,128)(2,1)S(1)}, bf16[3,1024,256]{2,1,0:T(8,128)(2,1)}, u32[]{:S(2)}) copy-start(bf16[3,1024,256]{2,1,0:T(8,128)(2,1)} %copy-done.2) | copy-start | bytes 4718596
  (6 other events, 7.8 us)

commit v2 on v1

--- a/solution.py
+++ b/solution.py
@@ -110,6 +110,8 @@
         ]
     )
     everyone = lax.all_gather(sums, axis)
+    everyone, early = lax.optimization_barrier((everyone, onward[0]))
+    onward = (early, onward[1])
     place = jnp.arange(count)
     behind = (me - 1 - place) % count
     ahead = (place - me - 1) % count
@@ -132,7 +134,6 @@
     rate = np.exp(-theta)
     fixed = np.stack([rate, rate / (1.0 + rate), np.sqrt(rate) / (1.0 + rate)]).astype(np.float32)
     coef = jnp.concatenate([jnp.asarray(fixed), jnp.stack([means, carry_up, carry_down])], axis=0)
-    coef, onward = lax.optimization_barrier((coef, onward))
     lanes = (rows // LANES, LANES)
     g, h = pl.pallas_call(
         line_kernel,
@@ -141,7 +142,7 @@
         out_specs=[pl.BlockSpec(memory_space=pltpu.VMEM)] * 2,
         compiler_params=pltpu.CompilerParams(vmem_limit_bytes=24 * 1024 * 1024),
         cost_estimate=pl.CostEstimate(
-            flops=10 * length * rows, bytes_accessed=12 * length * rows, transcendentals=0
+            flops=length * rows, bytes_accessed=length * rows, transcendentals=0
         ),
         name="line_solve",
     )(modes.reshape((length,) + lanes), coef.reshape((6,) + lanes))
@@ -382,7 +383,9 @@
     rise = jnp.einsum(
         "ky,zk->yz", sine.astype(jnp.bfloat16), rise_modes.astype(jnp.bfloat16), preferred_element_type=jnp.float32
     )
-    return jnp.stack([first, flux - rise, third - slope], axis=0), held, onward
+    second, third, late = lax.optimization_barrier((flux - rise, third - slope, onward[1]))
+    onward = jnp.concatenate([onward[0], late], axis=1)
+    return jnp.stack([first, second, third], axis=0), held, onward
 
 
 def body(velocity, mean_flow, chol_diag, chol_off, eddy_x, eddy_y, eddy_z, eddy_signs, tile_lists):
@@ -401,7 +404,8 @@
     near = lax.ppermute(keep, "gx", onward)
 
     def forward(held):
-        return lax.ppermute(held[0], "gx", onward)
+        middle = rows // 2
+        return tuple(lax.ppermute(part, "gx", onward) for part in (held[0][:, :middle], held[0][:, middle:]))
 
     inflow, (other, near), next_near = inlet_planes(
         mean_flow, chol_diag, chol_off, eddy_x, eddy_y, eddy_z, eddy_signs, columns, spanwise, (other, near), forward

time: 150 us -> 145 us (0.967)
  waiting for transfers between devices: 18.6 us -> 10.7 us
  starting transfers between devices: 8.58 us -> 12.1 us
  other arithmetic: 26 us -> 27.7 us
  local copies, waits for them, and re-layouts: 8.85 us -> 7.16 us
    ppermute x1 -> x2, waiting for transfers between devices: 17.9 us -> 4.82 us  [forward(): lax.ppermute(part, 'gx', onward)]
    add x0 -> x1, other arithmetic: none -> 3.6 us  [mix(): chol_off[1][:, None] * fl[0] + chol_off[2][:, None] * fl[1]]
    mul x1 -> x0, other arithmetic: 3.59 us -> none  [inlet_planes(): flux = second * (cells_y < rows - 1).astype(jnp.float32)[:, None]]
    ppermute x1 -> x2, starting transfers between devices: 3.62 us -> 7.09 us  [forward(): lax.ppermute(part, 'gx', onward)]
    unnamed x72 -> x61, local copies, waits for them, and re-layouts: 7.59 us -> 4.34 us
    ppermute x1, waiting for transfers between devices: 0.01 us -> 2.83 us  [body(): other = lax.ppermute(jnp.where(even, high, low), 'gx', swap)]
    convert_element_type x0 -> x1, other arithmetic: none -> 2.46 us  [inlet_planes(): cosine.astype(jnp.bfloat16)]
    sub x1 -> x0, other arithmetic: 2.44 us -> none  [wall_bases(): single(norm * np.cos(a))[:, None] * single(np.cos(b))[None]]
  transfers between devices with their start and end apart: 3 -> 4, of which waited for: 2 -> 3; matrix products, arithmetic and copies ran while one was open for 26% -> 26% of each run, Pallas kernels for 0% -> 2%
where the time goes in v2:
time: 145 us
  Pallas kernels  55.4 us (38%)
  other arithmetic  27.7 us (19%)
  matrix products  21 us (14%)
  starting transfers between devices  12.1 us (8%)
  waiting for transfers between devices  10.7 us (7%)
  local copies, waits for them, and re-layouts  7.16 us (5%)
  between operations  5.71 us (4%)
  blocking collectives  5.19 us (4%)
    pallas_call x1, Pallas kernels, march(): pl.pallas_call(functools.partial(march_kernel, slabs), out_shape=[jax.Sha...  52.8 us
    dot_general x2, matrix products, fluct_at(): jnp.einsum('ey,jez->jyz', shape_y, weight, preferred_element_type=jnp.flo...  10.6 us
    dot_general x1, matrix products, inlet_planes(): modes = jnp.einsum('yz,ky->zk', div, cosine, precision=high)  7.77 us
    ppermute x2, starting transfers between devices, forward(): lax.ppermute(part, 'gx', onward)  7.09 us
    all_gather x1, blocking collectives, line_solve(): everyone = lax.all_gather(sums, axis)  5.19 us
    ppermute x2, waiting for transfers between devices, forward(): lax.ppermute(part, 'gx', onward)  4.82 us
    unnamed x61, local copies, waits for them, and re-layouts  4.34 us
    select_n x1, other arithmetic, body(): keep = jnp.where(even, low, high)  3.82 us
  transfers between devices with their start and end apart: 4, of which 3 were waited for; matrix products, arithmetic and copies ran while one was open for 26% of the time, Pallas kernels for 2%

profile of v2, /device:TPU:8, one launch (start us, length us, event | category | flops | bytes accessed | tf_op | source)
XLA Modules:
  0.0 145.0 jit_solution(1509851148522020863)
XLA Ops:
  0.7 3.8 %broadcast_select_fusion.2 = (bf16[3,1024,256]{2,1,0:T(8,128)(2,1)}, bf16[3,1024,256]{2,1,0:T(8,128)(2,1)}) fusion(pred[]{:T(512)S(6)} %eq.53, bf16[3,1024,512]{2,1,0:T(8,128)(2,1)} %bitcast.102), kind=kLoop, calls=%fused_computation.49 | loop fusion | flops 1572864 | bytes 6291457 | tf_op jit(solution)/shard_map/jit(_where)/select_n | solution.py:402
  4.5 1.5 %collective-permute-start = (bf16[3,1024,256]{2,1,0:T(8,128)(2,1)}, bf16[3,1024,256]{2,1,0:T(8,128)(2,1)}, u32[]{:S(2)}, u32[]{:S(2)}) collective-permute-start(bf16[3,1024,256]{2,1,0:T(8,128)(2,1)} %get-tuple-element.54), channel_id=1, source_target_pairs={{0,4},{4,0},{8,12},{12,8},{16,20},{20,16},{24,28},{28,24},{1,5},{5... | collective-permute-start | bytes 4718600 | tf_op jit(solution)/shard_map/ppermute | solution.py:403
  6.0 3.5 %collective-permute-start.1 = (bf16[3,1024,256]{2,1,0:T(8,128)(2,1)}, bf16[3,1024,256]{2,1,0:T(8,128)(2,1)}, u32[]{:S(2)}, u32[]{:S(2)}) collective-permute-start(bf16[3,1024,256]{2,1,0:T(8,128)(2,1)} %get-tuple-element.53.keep_ref), channel_id=1, source_target_pairs={{0,8},{4,12},{8,16},{12,20},{16,24},{20,28},{1,9},{5,13},{9,17},{1... | collective-permute-start | bytes 4718600 | tf_op jit(solution)/shard_map/ppermute | solution.py:404
  9.6 2.1 %fusion.10 = f32[1536,512]{0,1:T(8,128)S(1)} fusion(s32[1536]{0:T(1024)S(1)} %copy-done.20, s32[512]{0:T(512)S(1)} %iota_add_fusion), kind=kLoop, calls=%fused_computation.20 | loop fusion | flops 15728640 | bytes 3153920 | tf_op jit(solution)/shard_map/mul | solution.py:28
  11.7 1.8 %fusion.13 = f32[3,1024]{1,0:T(4,128)S(1)} fusion(s32[1536]{0:T(1024)S(1)} %copy-done.29, f32[3,1536]{1,0:T(4,128)S(1)} %convert_multiply_fusion, f32[1536]{0:T(1024)S(1)} %fusion.43), kind=kOutput, calls=%fused_computation.25 | convolution fusion | flops 22029312 | bytes 43008 | tf_op jit(solution)/shard_map/ey,jez->jyz/dot_general | solution.py:361
  13.5 8.8 %fusion.14 = f32[3,1024,512]{2,1,0:T(8,128)} fusion(s32[1536]{0:T(1024)S(1)} %copy-done.29, f32[1536,512]{0,1:T(8,128)S(1)} %fusion.10, f32[3,1536]{1,0:T(4,128)S(1)} %convert_multiply_fusion), kind=kOutput, calls=%fused_computation.26 | convolution fusion | flops 4849139712 | bytes 9461760 | tf_op jit(solution)/shard_map/ey,jez->jyz/dot_general | solution.py:361
  22.7 3.6 %fusion.18 = (f32[1024,512]{1,0:T(8,128)S(1)}, f32[1024,512]{1,0:T(8,128)S(1)}) fusion(f32[3,1024,512]{2,1,0:T(8,128)} %fusion.14, f32[1024]{0:T(1024)S(1)} %bitcast.110, f32[1024]{0:T(1024)S(1)} %bitcast.108, f32[1024]{0:T(1024)S(1)} %bitcast.109, f32[1024]{0:T(1024)S(1)} %fusion.47, f32[1024]{0:T(1024)S(1)} %bitcast.111, f32[1024]{0:T(1024)S(1)} %bitcast.107), kind=kLoop, calls=%fused_computation.29 | loop fusion | flops 4718592 | bytes 10510336 | tf_op jit(solution)/shard_map/add | solution.py:367
  26.3 2.5 %select_convert_fusion = (bf16[32,32,1024]{2,1,0:T(8,128)(2,1)}, f32[32,32,1024]{2,1,0:T(8,128)S(1)}) fusion(pred[32,32]{1,0:T(8,128)(4,1)S(1)} %add_compare_fusion, f32[32,1024]{1,0:T(8,128)S(1)} %copy-done.13, f32[32,1024]{1,0:T(8,128)S(1)} %copy-done.14, f32[32,1024]{1,0:T(8,128)S(1)} %copy-done.15, f32[32,1024]{1,0:T(8,128)S(1)} %copy-done.16), kind=kLoop, calls=%fused_computation.10 | loop fusion | flops 5242880 | bytes 6816768 | tf_op jit(solution)/shard_map/convert_element_type | solution.py:381
  29.8 7.8 %multiply_reduce_fusion = (f32[16,1024]{1,0:T(8,128)S(1)}, f32[16,1024]{1,0:T(8,128)S(1)}, f32[512,1024]{1,0:T(8,128)S(1)}) fusion(f32[32,1024]{1,0:T(8,128)S(1)} %copy-done.7, f32[32,1024]{1,0:T(8,128)S(1)} %copy-done.8, f32[1024,1024]{1,0:T(8,128)S(1)} %bitcast_select_fusion, f32[1024,511]{1,0:T(8,128)S(1)} %bitcast.95, f32[1024,1]{1,0:T(8,128)S(1)} %copy.41, ...), kind=kOutput, calls=%fused_computation.40 | convolution fusion | flops 3225387008 | bytes 15071232 | tf_op jit(solution)/shard_map/yz,ky->zk/dot_general | solution.py:378
  38.1 2.8 %collective-permute-done.other_ref = bf16[3,1024,256]{2,1,0:T(8,128)(2,1)} collective-permute-done((bf16[3,1024,256]{2,1,0:T(8,128)(2,1)}, bf16[3,1024,256]{2,1,0:T(8,128)(2,1)}, u32[]{:S(2)}, u32[]{:S(2)}) %collective-permute-start) | collective-permute-done | bytes 1572896 | tf_op jit(solution)/shard_map/ppermute | solution.py:403
  40.9 3.1 %collective-permute-done.1.near_ref = bf16[3,1024,256]{2,1,0:T(8,128)(2,1)} collective-permute-done((bf16[3,1024,256]{2,1,0:T(8,128)(2,1)}, bf16[3,1024,256]{2,1,0:T(8,128)(2,1)}, u32[]{:S(2)}, u32[]{:S(2)}) %collective-permute-start.1) | collective-permute-done | bytes 1572896 | tf_op jit(solution)/shard_map/ppermute | solution.py:404
  44.0 2.4 %fusion.67 = (bf16[3,512,256]{2,1,0:T(8,128)(2,1)}, bf16[3,512,256]{2,1,0:T(8,128)(2,1)S(1)}) fusion(bf16[3,1024,256]{2,1,0:T(8,128)(2,1)} %collective-permute-done.other_ref), kind=kLoop, calls=%fused_computation.126 | loop fusion | bytes 3145728 | tf_op jit(solution)/shard_map/slice | solution.py:408
  46.5 3.6 %collective-permute-start.2 = (bf16[3,512,256]{2,1,0:T(8,128)(2,1)S(1)}, bf16[3,512,256]{2,1,0:T(8,128)(2,1)S(1)}, u32[]{:S(2)}, u32[]{:S(2)}) collective-permute-start(bf16[3,512,256]{2,1,0:T(8,128)(2,1)S(1)} %get-tuple-element.56), channel_id=1, source_target_pairs={{0,8},{4,12},{8,16},{12,20},{16,24},{20,28},{1,9},{5,13},{9,17},{1... | collective-permute-start | bytes 2359304 | tf_op jit(solution)/shard_map/ppermute | solution.py:408
  50.1 2.0 %add_convert_fusion = bf16[32,32,1024]{2,1,0:T(8,128)(2,1)} fusion(f32[32,1024]{1,0:T(8,128)S(1)} %copy-done.9, f32[32,1024]{1,0:T(8,128)S(1)} %copy-done.10, f32[32,1024]{1,0:T(8,128)S(1)} %copy-done.11, f32[32,1024]{1,0:T(8,128)S(1)} %copy-done.12), kind=kLoop, calls=%fused_computation.12 | loop fusion | flops 4194304 | bytes 2621440 | tf_op jit(solution)/shard_map/convert_element_type | solution.py:384
  52.1 3.3 %multiply_add_fusion = f32[1,1024,512]{2,1,0:T(8,128)} fusion(f32[3,1024,512]{2,1,0:T(8,128)} %fusion.14, f32[1024]{0:T(1024)S(1)} %bitcast.114, f32[1024]{0:T(1024)S(1)} %copy-done.22), kind=kLoop, calls=%fused_computation.45 | loop fusion | flops 1048576 | bytes 4202496 | tf_op jit(solution)/shard_map/add | solution.py:369
  55.4 3.5 %collective-permute-start.3 = (bf16[3,512,256]{2,1,0:T(8,128)(2,1)}, bf16[3,512,256]{2,1,0:T(8,128)(2,1)}, u32[]{:S(2)}, u32[]{:S(2)}) collective-permute-start(bf16[3,512,256]{2,1,0:T(8,128)(2,1)} %get-tuple-element.55), channel_id=1, source_target_pairs={{0,8},{4,12},{8,16},{12,20},{16,24},{20,28},{1,9},{5,13},{9,17},{1... | collective-permute-start | bytes 2359304 | tf_op jit(solution)/shard_map/ppermute | solution.py:408
  58.9 5.2 %all-gather.1 = f32[4,2,1024]{2,1,0:T(2,128)S(1)} all-gather(f32[1,2,1024]{2,1,0:T(2,128)S(1)} %maximum_bitcast_fusion.1), channel_id=2, replica_groups=mesh['gx'=8,'yz'=4] {'yz'}, dimensions={0}, use_global_device_ids=true | all-gather | bytes 40960 | tf_op jit(solution)/shard_map/all_gather | solution.py:112
  64.1 4.8 %collective-permute-done.2 = bf16[3,512,256]{2,1,0:T(8,128)(2,1)S(1)} collective-permute-done((bf16[3,512,256]{2,1,0:T(8,128)(2,1)S(1)}, bf16[3,512,256]{2,1,0:T(8,128)(2,1)S(1)}, u32[]{:S(2)}, u32[]{:S(2)}) %collective-permute-start.2) | collective-permute-done | bytes 786464 | tf_op jit(solution)/shard_map/ppermute | solution.py:408
  69.0 0.6 slice_reduce_fusion
  71.5 0.6 subtract_reduce_fusion
  72.3 0.7 fusion.55
  75.7 2.7 %line_solve.1 = (f32[512,8,128]{2,1,0:T(8,128)S(1)}, f32[512,8,128]{2,1,0:T(8,128)S(1)}) custom-call(f32[512,8,128]{2,1,0:T(8,128)S(1)} %bitcast.94, f32[6,8,128]{2,1,0:T(8,128)S(1)} %pad_maximum_fusion.2.coef_ref), custom_call_target="tpu_custom_call" | custom-call | flops 524288 | bytes 524288 | tf_op jit(solution)/shard_map/line_solve/pallas_call | solution.py:138
  78.7 1.3 copy-done.4
  80.0 0.6 copy-done.6
  80.7 1.3 convolution_subtract_fusion.1
  82.2 0.6 copy-done.5
  82.9 1.3 convolution_subtract_fusion
  84.5 0.6 pad_maximum_fusion
  85.1 3.4 %fusion.66 = f32[1,3,1024,512]{3,2,1,0:T(8,128)} fusion(f32[1,1024,512]{2,1,0:T(8,128)S(1)} %bitcast.100, f32[1,1024,512]{2,1,0:T(8,128)S(1)} %bitcast.98, f32[1,1024,512]{2,1,0:T(8,128)S(1)} %copy-done), kind=kLoop, calls=%fused_computation.125 | loop fusion | flops 3145728 | bytes 12582912 | tf_op jit(solution)/shard_map/broadcast_in_dim | solution.py:419
  88.7 1.2 pad_maximum_fusion.1.next_ref
  90.1 52.8 %march.1 = (bf16[3,1024,256]{2,1,0:T(8,128)(2,1)S(1)}, bf16[3,1024,256]{2,1,0:T(8,128)(2,1)S(1)}) custom-call(f32[1024,128]{1,0:T(8,128)S(1)} %broadcast_in_dim.34.mean_ref, bf16[3,1024,256]{2,1,0:T(8,128)(2,1)S(1)} %fusion.11.inlet_ref, bf16[3,1024,256]{2,1,0:T(8,128)(2,1)} %get-tuple-element.53.keep_ref, ...), custom_call_target="tpu_custom_call" | custom-call | flops 254803968 | bytes 11010048 | tf_op jit(solution)/shard_map/march/pallas_call | solution.py:325
  143.1 1.9 %maximum_bitcast_fusion = bf16[3,1,1024,512]{3,2,1,0:T(8,128)(2,1)} fusion(bf16[3,1024,256]{2,1,0:T(8,128)(2,1)S(1)} %get-tuple-element.52, bf16[3,1024,256]{2,1,0:T(8,128)(2,1)S(1)} %get-tuple-element.51), kind=kLoop, calls=%fused_computation.23 | loop fusion | flops 6291456 | bytes 6291456
  (84 shorter events, 3.6 us)
Async XLA Ops:
  0.6 8.8 %copy-start.26 = (s32[1536]{0:T(1024)S(1)}, s32[1536]{0:T(1024)}, u32[]{:S(2)}) copy-start(s32[1536]{0:T(1024)} %param.29) | copy-start | bytes 18436
  0.7 8.9 %copy-start.20 = (s32[1536]{0:T(1024)S(1)}, s32[1536]{0:T(1024)}, u32[]{:S(2)}) copy-start(s32[1536]{0:T(1024)} %param.31) | copy-start | bytes 18436
  4.5 7.2 %copy-start.21 = (s32[3,1536]{1,0:T(4,128)S(1)}, s32[3,1536]{1,0:T(4,128)}, u32[]{:S(2)}) copy-start(s32[3,1536]{1,0:T(4,128)} %param.32) | copy-start | bytes 55300
  4.5 7.2 %copy-start.29 = (s32[1536]{0:T(1024)S(1)}, s32[1536]{0:T(1024)}, u32[]{:S(2)}) copy-start(s32[1536]{0:T(1024)} %param.30) | copy-start | bytes 18436
  4.5 36.5 %collective-permute-start = (bf16[3,1024,256]{2,1,0:T(8,128)(2,1)}, bf16[3,1024,256]{2,1,0:T(8,128)(2,1)}, u32[]{:S(2)}, u32[]{:S(2)}) collective-permute-start(bf16[3,1024,256]{2,1,0:T(8,128)(2,1)} %get-tuple-element.54), channel_id=1, source_target_pairs={{0,4},{4,0},{8,12},{12,8},{16,20},{20,16},{24,28},{28,24},{1,5},{5... | collective-permute-start | bytes 4718600 | tf_op jit(solution)/shard_map/ppermute | solution.py:403
  6.0 38.1 %collective-permute-start.1 = (bf16[3,1024,256]{2,1,0:T(8,128)(2,1)}, bf16[3,1024,256]{2,1,0:T(8,128)(2,1)}, u32[]{:S(2)}, u32[]{:S(2)}) collective-permute-start(bf16[3,1024,256]{2,1,0:T(8,128)(2,1)} %get-tuple-element.53.keep_ref), channel_id=1, source_target_pairs={{0,8},{4,12},{8,16},{12,20},{16,24},{20,28},{1,9},{5,13},{9,17},{1... | collective-permute-start | bytes 4718600 | tf_op jit(solution)/shard_map/ppermute | solution.py:404
  13.5 8.8 %copy-start.24 = (f32[3,1024]{1,0:T(4,128)S(1)}, f32[3,1024]{1,0:T(4,128)}, u32[]{:S(2)}) copy-start(f32[3,1024]{1,0:T(4,128)} %param.27) | copy-start | bytes 36868
  13.5 8.8 %copy-start.25 = (f32[3,1024]{1,0:T(4,128)S(1)}, f32[3,1024]{1,0:T(4,128)}, u32[]{:S(2)}) copy-start(f32[3,1024]{1,0:T(4,128)} %param.28) | copy-start | bytes 36868
  22.6 3.7 %copy-start.13 = (f32[32,1024]{1,0:T(8,128)S(1)}, f32[32,1024]{1,0:T(8,128)}, u32[]{:S(2)}) copy-start(f32[32,1024]{1,0:T(8,128)} %constant.176.clone) | copy-start | bytes 393220
  22.6 3.7 %copy-start.14 = (f32[32,1024]{1,0:T(8,128)S(1)}, f32[32,1024]{1,0:T(8,128)}, u32[]{:S(2)}) copy-start(f32[32,1024]{1,0:T(8,128)} %constant.175.clone) | copy-start | bytes 393220
  22.6 3.7 %copy-start.15 = (f32[32,1024]{1,0:T(8,128)S(1)}, f32[32,1024]{1,0:T(8,128)}, u32[]{:S(2)}) copy-start(f32[32,1024]{1,0:T(8,128)} %constant.174.clone) | copy-start | bytes 393220
  22.7 3.7 %copy-start.16 = (f32[32,1024]{1,0:T(8,128)S(1)}, f32[32,1024]{1,0:T(8,128)}, u32[]{:S(2)}) copy-start(f32[32,1024]{1,0:T(8,128)} %constant.173.clone) | copy-start | bytes 393220
  26.3 2.8 %copy-start.1 = (f32[1024,512]{1,0:T(8,128)}, f32[1024,512]{1,0:T(8,128)S(1)}, u32[]{:S(2)}) copy-start(f32[1024,512]{1,0:T(8,128)S(1)} %get-tuple-element.49) | copy-start | bytes 6291460
  26.3 2.8 %copy-start.3 = (f32[1024,512]{1,0:T(8,128)}, f32[1024,512]{1,0:T(8,128)S(1)}, u32[]{:S(2)}) copy-start(f32[1024,512]{1,0:T(8,128)S(1)} %get-tuple-element.50) | copy-start | bytes 6291460
  37.5 12.5 %copy-start.9 = (f32[32,1024]{1,0:T(8,128)S(1)}, f32[32,1024]{1,0:T(8,128)}, u32[]{:S(2)}) copy-start(f32[32,1024]{1,0:T(8,128)} %constant.180.clone) | copy-start | bytes 393220
  37.6 12.5 %copy-start.10 = (f32[32,1024]{1,0:T(8,128)S(1)}, f32[32,1024]{1,0:T(8,128)}, u32[]{:S(2)}) copy-start(f32[32,1024]{1,0:T(8,128)} %constant.179.clone) | copy-start | bytes 393220
  37.6 12.5 %copy-start.11 = (f32[32,1024]{1,0:T(8,128)S(1)}, f32[32,1024]{1,0:T(8,128)}, u32[]{:S(2)}) copy-start(f32[32,1024]{1,0:T(8,128)} %constant.178.clone) | copy-start | bytes 393220
  37.6 12.5 %copy-start.12 = (f32[32,1024]{1,0:T(8,128)S(1)}, f32[32,1024]{1,0:T(8,128)}, u32[]{:S(2)}) copy-start(f32[32,1024]{1,0:T(8,128)} %constant.177.clone) | copy-start | bytes 393220
  38.1 14.0 %copy-start.22 = (f32[1024]{0:T(1024)S(1)}, f32[1024]{0:T(1024)}, u32[]{:S(2)}) copy-start(f32[1024]{0:T(1024)} %param.26) | copy-start | bytes 12292
  46.4 12.4 %copy-start.17 = (f32[16,1024]{1,0:T(8,128)S(1)}, f32[16,1024]{1,0:T(8,128)}, u32[]{:S(2)}) copy-start(f32[16,1024]{1,0:T(8,128)} %constant.185.clone) | copy-start | bytes 196612
  46.4 12.4 %copy-start.18 = (f32[16,1024]{1,0:T(8,128)S(1)}, f32[16,1024]{1,0:T(8,128)}, u32[]{:S(2)}) copy-start(f32[16,1024]{1,0:T(8,128)} %constant.184.clone) | copy-start | bytes 196612
  46.4 12.5 %copy-start.19 = (f32[16,1024]{1,0:T(8,128)S(1)}, f32[16,1024]{1,0:T(8,128)}, u32[]{:S(2)}) copy-start(f32[16,1024]{1,0:T(8,128)} %constant.183.clone) | copy-start | bytes 196612
  46.4 29.2 %copy-start.27 = (f32[1024]{0:T(1024)S(1)}, f32[1024]{0:T(1024)}, u32[]{:S(2)}) copy-start(f32[1024]{0:T(1024)} %constant.193) | copy-start | bytes 12292
  46.4 29.3 %copy-start.28 = (f32[1024]{0:T(1024)S(1)}, f32[1024]{0:T(1024)}, u32[]{:S(2)}) copy-start(f32[1024]{0:T(1024)} %constant.187.clone) | copy-start | bytes 12292
  46.4 29.3 %copy-start.23 = (f32[3,8,128]{2,1,0:T(8,128)S(1)}, f32[3,8,128]{2,1,0:T(8,128)}, u32[]{:S(2)}) copy-start(f32[3,8,128]{2,1,0:T(8,128)} %constant.192) | copy-start | bytes 36868
  46.5 22.5 %collective-permute-start.2 = (bf16[3,512,256]{2,1,0:T(8,128)(2,1)S(1)}, bf16[3,512,256]{2,1,0:T(8,128)(2,1)S(1)}, u32[]{:S(2)}, u32[]{:S(2)}) collective-permute-start(bf16[3,512,256]{2,1,0:T(8,128)(2,1)S(1)} %get-tuple-element.56), channel_id=1, source_target_pairs={{0,8},{4,12},{8,16},{12,20},{16,24},{20,28},{1,9},{5,13},{9,17},{1... | collective-permute-start | bytes 2359304 | tf_op jit(solution)/shard_map/ppermute | solution.py:408
  55.4 28.8 %collective-permute-start.3 = (bf16[3,512,256]{2,1,0:T(8,128)(2,1)}, bf16[3,512,256]{2,1,0:T(8,128)(2,1)}, u32[]{:S(2)}, u32[]{:S(2)}) collective-permute-start(bf16[3,512,256]{2,1,0:T(8,128)(2,1)} %get-tuple-element.55), channel_id=1, source_target_pairs={{0,8},{4,12},{8,16},{12,20},{16,24},{20,28},{1,9},{5,13},{9,17},{1... | collective-permute-start | bytes 2359304 | tf_op jit(solution)/shard_map/ppermute | solution.py:408
  78.4 1.6 %copy-start.4 = (f32[1024,512]{1,0:T(8,128)S(1)}, f32[1024,512]{1,0:T(8,128)}, u32[]{:S(2)}) copy-start(f32[1024,512]{1,0:T(8,128)} %copy-done.3) | copy-start | bytes 6291460
  78.4 2.2 %copy-start.6 = (bf16[32,32,1024]{2,1,0:T(8,128)(2,1)S(1)}, bf16[32,32,1024]{2,1,0:T(8,128)(2,1)}, u32[]{:S(2)}) copy-start(bf16[32,32,1024]{2,1,0:T(8,128)(2,1)} %add_convert_fusion) | copy-start | bytes 6291460
  80.7 1.6 %copy-start.2 = (f32[1024,512]{1,0:T(8,128)S(1)}, f32[1024,512]{1,0:T(8,128)}, u32[]{:S(2)}) copy-start(f32[1024,512]{1,0:T(8,128)} %copy-done.1) | copy-start | bytes 6291460
  80.7 2.2 %copy-start.5 = (bf16[32,32,1024]{2,1,0:T(8,128)(2,1)S(1)}, bf16[32,32,1024]{2,1,0:T(8,128)(2,1)}, u32[]{:S(2)}) copy-start(bf16[32,32,1024]{2,1,0:T(8,128)(2,1)} %get-tuple-element.57) | copy-start | bytes 6291460
  82.9 1.6 %copy-start = (f32[1,1024,512]{2,1,0:T(8,128)S(1)}, f32[1,1024,512]{2,1,0:T(8,128)}, u32[]{:S(2)}) copy-start(f32[1,1024,512]{2,1,0:T(8,128)} %multiply_add_fusion) | copy-start | bytes 6291460
  (2 other events, 1.9 us)
